TPU v7x, 128 devices: a whole 4x4x4 slice. The times are simulated.
128 devices in a mesh: xs: 4 (over x), bx: 32 (over z, y, core).
Axes of the slice: x: 4, y: 4, z: 4, core: 2. Of those that a mesh axis runs over, the one named last changes fastest.
Arguments:
- state: float32 [4, 256, 14, 16, 256], P('xs', 'bx'), may hold values from -6 to 6
- diffusivity: float32 [4, 256, 16, 256], P('xs', 'bx'), may hold values from 0.5 to 2
- velocity: float32 [4, 256, 3, 16, 256], P('xs', 'bx'), may hold values from -1 to 1
- species_scale: float32 [14], replicated, may hold values from 0.5 to 2
- new_owner: int32 [256], replicated, may hold values from 0 to 31, as said below
Outputs:
- advanced: float32 [4, 1280, 14, 16, 256], P('xs', 'bx')
Inputs may be any that keep to these rules, and one draw needn't show every extreme that they name: `new_owner`: box b starts at owner b // 8. No two boxes of one starting owner go to the same other owner, and in every draw some owner receives a box from every other starting owner.
All inputs are finite; a program needn't handle non-finite values.
Results may differ from a plain program's by a relative error of at most 0.00002.
Values sent between devices are 32-bit elements; how exact they have to be, the bound alone decides.
A program may use at most 384 MiB of HBM per device.

v0:
```python
import math

import jax
import jax.numpy as jnp
from jax import lax
from jax.sharding import PartitionSpec as P

time_step = 0.03


def extended(cells, sides, width):
    for axis, dim in sides:
        count = lax.axis_size(axis)
        head = lax.slice_in_dim(cells, 0, width, axis=dim)
        tail = lax.slice_in_dim(cells, cells.shape[dim] - width, cells.shape[dim], axis=dim)
        cells = jnp.concatenate(
            [
                lax.ppermute(tail, axis, [(i, (i + 1) % count) for i in range(count)]),
                cells,
                lax.ppermute(head, axis, [((i + 1) % count, i) for i in range(count)]),
            ],
            axis=dim,
        )
    return cells


def neighbours(field, side):
    lanes = field.shape[-1]
    coord = lax.broadcasted_iota(jnp.int32, (lanes,), 0) % side
    up_y = jnp.concatenate([field[..., side:], field[..., lanes - side :]], axis=-1)
    down_y = jnp.concatenate([field[..., :side], field[..., : lanes - side]], axis=-1)
    up_z = jnp.concatenate([field[..., 1:], field[..., lanes - 1 :]], axis=-1)
    down_z = jnp.concatenate([field[..., :1], field[..., : lanes - 1]], axis=-1)
    up_z = jnp.where(coord == side - 1, field, up_z)
    down_z = jnp.where(coord == 0, field, down_z)
    return (up_y, down_y, up_z, down_z)


def advance(conserved, diffusivity, velocity, scale):
    side = math.isqrt(conserved.shape[-1])
    center = conserved[..., 1:-1, :]
    ahead = conserved[..., 2:, :]
    behind = conserved[..., :-2, :]
    kappa = diffusivity[..., 1:-1, :]
    kappa_ahead = diffusivity[..., 2:, :]
    kappa_behind = diffusivity[..., :-2, :]
    q_up_y, q_down_y, q_up_z, q_down_z = neighbours(center, side)
    k_up_y, k_down_y, k_up_z, k_down_z = neighbours(kappa, side)
    spread = (kappa + kappa_ahead) * (ahead - center) + (kappa + kappa_behind) * (behind - center)
    spread = (
        spread + (kappa + k_up_y) * (q_up_y - center) + (kappa + k_down_y) * (q_down_y - center)
    )
    spread = (
        spread + (kappa + k_up_z) * (q_up_z - center) + (kappa + k_down_z) * (q_down_z - center)
    )
    spread = 0.5 * spread
    flow = velocity[..., 1:-1, :]
    along_x = flow[..., 0:1, :, :]
    along_y = flow[..., 1:2, :, :]
    along_z = flow[..., 2:3, :, :]
    transport = jnp.maximum(along_x, 0.0) * (center - behind) + jnp.minimum(along_x, 0.0) * (
        ahead - center
    )
    transport = (
        transport
        + jnp.maximum(along_y, 0.0) * (center - q_down_y)
        + jnp.minimum(along_y, 0.0) * (q_up_y - center)
    )
    transport = (
        transport
        + jnp.maximum(along_z, 0.0) * (center - q_down_z)
        + jnp.minimum(along_z, 0.0) * (q_up_z - center)
    )
    return center + time_step * (scale * spread - transport)


def two_steps(stacked, fields, scale):
    edged = extended(stacked, (("xs", 2),), 1)
    kappa = edged[:, fields : fields + 1]
    flow = edged[:, fields + 1 :]
    first = advance(edged[:, :fields], kappa, flow, scale)
    again = extended(first, (("xs", 2),), 1)
    return advance(again, kappa, flow, scale)


def on_device(state, diffusivity, velocity, species_scale, new_owner):
    owners = lax.axis_size("bx")
    here = lax.axis_index("bx")
    holding = state.shape[1]
    fields = state.shape[2]
    scale = species_scale[:, None, None]
    local_owner = lax.dynamic_slice_in_dim(new_owner, here * holding, holding)
    moving = local_owner != here
    targets = jnp.arange(owners, dtype=jnp.int32)
    picked = (local_owner[None, :] == targets[:, None]) & moving[None, :]
    source_slot = jnp.sum(
        jnp.where(picked, jnp.arange(holding, dtype=jnp.int32)[None, :], 0), axis=1
    )
    present = jnp.any(picked, axis=1)
    staying = jnp.logical_not(moving).reshape(holding, 1, 1, 1)
    stacked = jnp.concatenate([state[0], diffusivity[0][:, None], velocity[0]], axis=1)
    chosen = jnp.take(stacked, source_slot, axis=0)
    arrived = lax.all_to_all(
        jnp.where(present.reshape(owners, 1, 1, 1), chosen, 0.0),
        "bx",
        split_axis=0,
        concat_axis=0,
        tiled=True,
    )
    holdings = jnp.concatenate([jnp.where(staying, stacked, 0.0), arrived], axis=0)
    result = two_steps(holdings, fields, scale)
    return result[None]


def solution(mesh):
    in_specs = (
        P("xs", "bx", None, None, None),
        P("xs", "bx", None, None),
        P("xs", "bx", None, None, None),
        P(),
        P(),
    )
    out_specs = P("xs", "bx", None, None, None)
    return jax.shard_map(
        on_device, mesh=mesh, in_specs=in_specs, out_specs=out_specs, check_vma=False
    )
```

profile of v0, /device:TPU:6, one launch (start us, length us, event | category | flops | bytes accessed | tf_op | source)
XLA Modules:
  0.0 316.6 jit_solution(13774301124902221113)
XLA Ops:
  1.0 3.6 %broadcast_select_fusion = (f32[8,18,16,256]{3,2,1,0:T(8,128)S(1)}, f32[8,18,16,256]{3,2,1,0:T(8,128)}) fusion(pred[8]{0:T(512)(128)(4,1)S(1)} %get-tuple-element.13, f32[8,3,16,256]{3,2,1,0:T(8,128)} %bitcast.36, f32[8,1,16,256]{3,2,1,0:T(8,128)} %bitcast.37, f32[8,14,16,256]{3,2,1,0:T(8,128)} %bitcast.35), kind=kLoop, calls=%fused_computation.104 | loop fusion | flops 1769472 | bytes 7077896 | tf_op jit(solution)/shard_map/jit(_where)/select_n | solution.py:110
  4.6 6.4 %gather_fusion = f32[32,18,16,256]{3,2,1,0:T(8,128)} fusion(f32[8,18,16,256]{3,2,1,0:T(8,128)} %get-tuple-element.50, s32[1024]{0:T(1024)S(1)} %pad_clamp_fusion), kind=kCustom, calls=%fused_computation | custom fusion | bytes 18874496 | tf_op jit(solution)/shard_map/jit(_take)/gather | solution.py:102
  11.0 9.4 %select_select_fusion = f32[32,18,16,256]{3,2,1,0:T(8,128)} fusion(f32[32,18,16,256]{3,2,1,0:T(8,128)} %gather_fusion, pred[32]{0:T(512)(128)(4,1)S(1)} %compare_and_fusion, pred[32]{0:T(512)(128)(4,1)S(1)} %fusion.61), kind=kLoop, calls=%fused_computation.51 | loop fusion | flops 4718592 | bytes 18874432 | tf_op jit(solution)/shard_map/jit(_where)/select_n | solution.py:104
  20.5 8.6 %all-to-all-start = ((f32[32,18,16,256]{3,2,1,0:T(8,128)}), f32[32,18,16,256]{3,2,1,0:T(8,128)}, u32[]{:S(2)}, u32[]{:S(2)}) async-start(f32[32,18,16,256]{3,2,1,0:T(8,128)} %select_select_fusion), calls=%async_computation | async-start | bytes 18874368 | tf_op jit(solution)/shard_map/all_to_all | solution.py:103
  29.1 119.2 %all-to-all-done = f32[32,18,16,256]{3,2,1,0:T(8,128)} async-done(((f32[32,18,16,256]{3,2,1,0:T(8,128)}), f32[32,18,16,256]{3,2,1,0:T(8,128)}, u32[]{:S(2)}, u32[]{:S(2)}) %all-to-all-start) | async-done | bytes 9437216 | tf_op jit(solution)/shard_map/all_to_all | solution.py:103
  148.3 4.4 %fusion.41 = (f32[40,18,1,256]{3,2,1,0:T(1,128)S(1)}, f32[40,18,1,256]{3,2,1,0:T(1,128)S(1)}) fusion(f32[32,18,16,256]{3,2,1,0:T(8,128)} %all-to-all-done, f32[8,18,16,256]{3,2,1,0:T(8,128)S(1)} %get-tuple-element.49), kind=kLoop, calls=%fused_computation.107 | loop fusion | flops 368640 | bytes 13271040 | tf_op jit(solution)/shard_map/concatenate | solution.py:110
  153.6 2.4 collective-permute-start.1
  157.2 1.6 fusion.47
  158.7 1.6 fusion.45
  160.3 11.2 %fusion.20 = (f32[40,14,16,240]{3,2,1,0:T(8,128)}, f32[40,14,16,240]{3,2,1,0:T(8,128)}) fusion(f32[32,18,16,256]{3,2,1,0:T(8,128)} %all-to-all-done, f32[8,18,16,256]{3,2,1,0:T(8,128)S(1)} %get-tuple-element.49), kind=kLoop, calls=%fused_computation.72 | loop fusion | flops 4300800 | bytes 28999680 | tf_op jit(solution)/shard_map/concatenate | solution.py:110
  171.5 11.5 %fusion.22 = (f32[40,14,16,255]{3,2,1,0:T(8,128)}, f32[40,14,16,255]{3,2,1,0:T(8,128)}) fusion(f32[32,18,16,256]{3,2,1,0:T(8,128)} %all-to-all-done, f32[8,18,16,256]{3,2,1,0:T(8,128)S(1)} %get-tuple-element.49), kind=kLoop, calls=%fused_computation.74 | loop fusion | flops 4569600 | bytes 30074880 | tf_op jit(solution)/shard_map/concatenate | solution.py:110
  184.2 6.5 %fusion.39 = (f32[40,14,16,1]{3,2,1,0:T(8,128)}, f32[40,14,16,1]{3,2,1,0:T(8,128)}) fusion(f32[32,18,16,256]{3,2,1,0:T(8,128)} %all-to-all-done, f32[8,18,16,256]{3,2,1,0:T(8,128)S(1)} %get-tuple-element.49), kind=kLoop, calls=%fused_computation.101 | loop fusion | flops 17920 | bytes 11868160 | tf_op jit(solution)/shard_map/concatenate | solution.py:110
  190.7 6.5 %fusion.37 = (f32[40,14,16,16]{3,2,1,0:T(8,128)}, f32[40,14,16,16]{3,2,1,0:T(8,128)}) fusion(f32[32,18,16,256]{3,2,1,0:T(8,128)} %all-to-all-done, f32[8,18,16,256]{3,2,1,0:T(8,128)S(1)} %get-tuple-element.49), kind=kLoop, calls=%fused_computation.99 | loop fusion | flops 286720 | bytes 12943360 | tf_op jit(solution)/shard_map/concatenate | solution.py:110
  197.2 3.3 %fusion.53 = (f32[40,16,256]{2,1,0:T(8,128)S(1)}, f32[40,1,16,256]{3,2,1,0:T(8,128)S(1)}, f32[40,16,256]{2,1,0:T(8,128)}, f32[40,1,16,256]{3,2,1,0:T(8,128)S(1)}...) fusion(f32[40,18,1,256]{3,2,1,0:T(1,128)S(1)} %collective-permute-done, f32[32,18,16,256]{3,2,1,0:T(8,128)} %all-to-all-done, ...), kind=kLoop, calls=%fused_computation.122 | loop fusion | flops 1310720 | bytes 16465920 | tf_op jit(solution)/shard_map/mul | solution.py:49
  201.4 2.8 maximum_bitcast_fusion.2
  205.1 2.4 fusion.54
  207.5 36.7 %fusion.5 = f32[40,14,16,256]{3,2,1,0:T(8,128)} fusion(f32[40,14,16,255]{3,2,1,0:T(8,128)} %get-tuple-element.36, f32[40,14,16,1]{3,2,1,0:T(8,128)} %get-tuple-element.38, f32[40,14,16,1]{3,2,1,0:T(8,128)} %get-tuple-element.37, f32[40,14,16,255]{3,2,1,0:T(8,128)} %get-tuple-element.35, f32[40,14,16,240]{3,2,1,0:T(8,128)} %get-tuple-element.32, ...), kind=kLoop, calls=%fused_computation.57 | loop fusion | flops 105512960 | bytes 67011128 | tf_op jit(solution)/shard_map/add | solution.py:74
  244.2 4.8 %fusion.67 = (f32[40,14,1,256]{3,2,1,0:T(1,128)S(1)}, f32[40,14,1,256]{3,2,1,0:T(1,128)S(1)}) fusion(f32[40,14,16,256]{3,2,1,0:T(8,128)} %fusion.5), kind=kLoop, calls=%fused_computation.152 | loop fusion | bytes 2293760 | tf_op jit(solution)/shard_map/slice | solution.py:14
  249.1 14.2 %fusion.70 = (f32[40,14,16,255]{3,2,1,0:T(8,128)}, f32[40,14,16,255]{3,2,1,0:T(8,128)}) fusion(f32[40,14,16,256]{3,2,1,0:T(8,128)} %fusion.5), kind=kLoop, calls=%fused_computation.155 | loop fusion | bytes 36556800 | tf_op jit(solution)/shard_map/slice | solution.py:32
  263.3 8.0 %fusion.68 = (f32[40,14,16,240]{3,2,1,0:T(8,128)}, f32[40,14,16,240]{3,2,1,0:T(8,128)}) fusion(f32[40,14,16,256]{3,2,1,0:T(8,128)S(1)} %bitcast.34), kind=kLoop, calls=%fused_computation.153 | loop fusion | bytes 34406400 | tf_op jit(solution)/shard_map/slice | solution.py:30
  271.4 3.2 %collective-permute-start.3 = (f32[40,14,1,256]{3,2,1,0:T(1,128)S(1)}, f32[40,14,1,256]{3,2,1,0:T(1,128)S(1)}, u32[]{:S(2)}, u32[]{:S(2)}) collective-permute-start(f32[40,14,1,256]{3,2,1,0:T(1,128)S(1)} %get-tuple-element.40), channel_id=1, source_target_pairs={{0,32},{32,64},{64,96},{96,0},{1,33},{33,65},{65,97},{97,1},{2,34}... | collective-permute-start | bytes 1720328 | tf_op jit(solution)/shard_map/ppermute | solution.py:18
  274.6 5.4 %fusion.69 = (f32[40,14,16,16]{3,2,1,0:T(8,128)}, f32[40,14,16,16]{3,2,1,0:T(8,128)}) fusion(f32[40,14,16,256]{3,2,1,0:T(8,128)S(1)} %bitcast.34), kind=kLoop, calls=%fused_computation.154 | loop fusion | bytes 2293760 | tf_op jit(solution)/shard_map/slice | solution.py:30
  279.9 5.2 %fusion.71 = (f32[40,14,16,1]{3,2,1,0:T(8,128)}, f32[40,14,16,1]{3,2,1,0:T(8,128)}) fusion(f32[40,14,16,256]{3,2,1,0:T(8,128)S(1)} %bitcast.34), kind=kLoop, calls=%fused_computation.156 | loop fusion | bytes 143360 | tf_op jit(solution)/shard_map/slice | solution.py:32
  286.8 29.6 %fusion.15 = f32[1,40,14,16,256]{4,3,2,1,0:T(8,128)} fusion(f32[40,14,16,256]{3,2,1,0:T(8,128)S(1)} %bitcast.34, f32[40,14,1,256]{3,2,1,0:T(1,128)} %copy-done.3, f32[40,14,16,255]{3,2,1,0:T(8,128)} %get-tuple-element.46, f32[40,14,16,1]{3,2,1,0:T(8,128)} %get-tuple-element.48, f32[40,14,16,1]{3,2,1,0:T(8,128)} %get-tuple-element.47, ...), kind=kLoop, calls=%fused_computation.67 | loop fusion | flops 98631680 | bytes 64062008 | tf_op jit(solution)/shard_map/broadcast_in_dim | solution.py:112
  (36 shorter events, 7.7 us)
Async XLA Ops:
  20.4 8.6 %copy-start.4 = (f32[14]{0:T(128)S(1)}, f32[14]{0:T(128)}, u32[]{:S(2)}) copy-start(f32[14]{0:T(128)} %param.8) | copy-start | bytes 172
  20.5 127.8 %all-to-all-start = ((f32[32,18,16,256]{3,2,1,0:T(8,128)}), f32[32,18,16,256]{3,2,1,0:T(8,128)}, u32[]{:S(2)}, u32[]{:S(2)}) async-start(f32[32,18,16,256]{3,2,1,0:T(8,128)} %select_select_fusion), calls=%async_computation | async-start | bytes 18874368 | tf_op jit(solution)/shard_map/all_to_all | solution.py:103
  152.7 44.5 %collective-permute-start = (f32[40,18,1,256]{3,2,1,0:T(1,128)S(1)}, f32[40,18,1,256]{3,2,1,0:T(1,128)S(1)}, u32[]{:S(2)}, u32[]{:S(2)}) collective-permute-start(f32[40,18,1,256]{3,2,1,0:T(1,128)S(1)} %get-tuple-element.29), channel_id=1, source_target_pairs={{32,0},{64,32},{96,64},{0,96},{33,1},{65,33},{97,65},{1,97},{34,2}... | collective-permute-start | bytes 2211848 | tf_op jit(solution)/shard_map/ppermute | solution.py:20
  153.6 47.8 %collective-permute-start.1 = (f32[40,18,1,256]{3,2,1,0:T(1,128)S(1)}, f32[40,18,1,256]{3,2,1,0:T(1,128)S(1)}, u32[]{:S(2)}, u32[]{:S(2)}) collective-permute-start(f32[40,18,1,256]{3,2,1,0:T(1,128)S(1)} %get-tuple-element.30), channel_id=1, source_target_pairs={{0,32},{32,64},{64,96},{96,0},{1,33},{33,65},{65,97},{97,1},{2,34}... | collective-permute-start | bytes 2211848 | tf_op jit(solution)/shard_map/ppermute | solution.py:18
  197.2 7.0 %copy-start = (f32[40,18,1,256]{3,2,1,0:T(1,128)}, f32[40,18,1,256]{3,2,1,0:T(1,128)S(1)}, u32[]{:S(2)}) copy-start(f32[40,18,1,256]{3,2,1,0:T(1,128)S(1)} %collective-permute-done) | copy-start | bytes 2211844
  201.4 6.1 %copy-start.1 = (f32[40,18,1,256]{3,2,1,0:T(1,128)}, f32[40,18,1,256]{3,2,1,0:T(1,128)S(1)}, u32[]{:S(2)}) copy-start(f32[40,18,1,256]{3,2,1,0:T(1,128)S(1)} %collective-permute-done.1) | copy-start | bytes 2211844
  244.2 19.1 %slice-start = ((s8[9175040]{0:T(1024)(128)(4,1)}), s8[4194304]{0:T(1024)(128)(4,1)S(1)}, s32[]{:S(2)}) async-start(s8[9175040]{0:T(1024)(128)(4,1)} %bitcast.33), calls=%async_computation.1 | async-start | bytes 8388608
  249.0 14.3 %slice-start.1 = ((s8[9175040]{0:T(1024)(128)(4,1)}), s8[4194304]{0:T(1024)(128)(4,1)S(1)}, s32[]{:S(2)}) async-start(s8[9175040]{0:T(1024)(128)(4,1)} %bitcast.33), calls=%async_computation.2 | async-start | bytes 8388608
  249.0 14.2 %slice-start.2 = ((s8[9175040]{0:T(1024)(128)(4,1)}), s8[786432]{0:T(1024)(128)(4,1)S(1)}, s32[]{:S(2)}) async-start(s8[9175040]{0:T(1024)(128)(4,1)} %bitcast.33), calls=%async_computation.3 | async-start | bytes 1572864
  271.4 13.8 %collective-permute-start.2 = (f32[40,14,1,256]{3,2,1,0:T(1,128)S(1)}, f32[40,14,1,256]{3,2,1,0:T(1,128)S(1)}, u32[]{:S(2)}, u32[]{:S(2)}) collective-permute-start(f32[40,14,1,256]{3,2,1,0:T(1,128)S(1)} %get-tuple-element.39), channel_id=1, source_target_pairs={{32,0},{64,32},{96,64},{0,96},{33,1},{65,33},{97,65},{1,97},{34,2}... | collective-permute-start | bytes 1720328 | tf_op jit(solution)/shard_map/ppermute | solution.py:20
  271.4 13.8 %collective-permute-start.3 = (f32[40,14,1,256]{3,2,1,0:T(1,128)S(1)}, f32[40,14,1,256]{3,2,1,0:T(1,128)S(1)}, u32[]{:S(2)}, u32[]{:S(2)}) collective-permute-start(f32[40,14,1,256]{3,2,1,0:T(1,128)S(1)} %get-tuple-element.40), channel_id=1, source_target_pairs={{0,32},{32,64},{64,96},{96,0},{1,33},{33,65},{65,97},{97,1},{2,34}... | collective-permute-start | bytes 1720328 | tf_op jit(solution)/shard_map/ppermute | solution.py:18
  285.2 0.8 copy-start.2
  286.0 0.8 copy-start.3
where the time goes:
time: 317 us
  other arithmetic  136 us (43%)
  waiting for transfers between devices  119 us (38%)
  local copies, waits for them, and re-layouts  45.7 us (14%)
  starting transfers between devices  15.1 us (5%)
    all_to_all x1, waiting for transfers between devices, on_device(): lax.all_to_all(jnp.where(present.reshape(owners, 1, 1, 1), chosen, 0.0),...  119 us
    concatenate x9, other arithmetic, on_device(): jnp.concatenate([jnp.where(staying, stacked, 0.0), arrived], axis=0)  45.6 us
    add x1, other arithmetic, advance(): return center + time_step * (scale * spread - transport)  36.7 us
    broadcast_in_dim x1, other arithmetic, on_device(): return result[None]  29.6 us
    slice x2, local copies, waits for them, and re-layouts, neighbours(): up_z = jnp.concatenate([field[..., 1:], field[..., lanes - 1:]], axis=-1)  19.4 us
    select_n x1, other arithmetic, on_device(): jnp.where(present.reshape(owners, 1, 1, 1), chosen, 0.0)  9.43 us
    all_to_all x1, starting transfers between devices, on_device(): lax.all_to_all(jnp.where(present.reshape(owners, 1, 1, 1), chosen, 0.0),...  8.58 us
    slice x1, local copies, waits for them, and re-layouts, neighbours(): field[..., side:]  8.05 us
  transfers between devices with their start and end apart: 5, of which 1 were waited for; matrix products, arithmetic and copies ran while one was open for 18% of the time, Pallas kernels for 0%

commit v1 on v0

v1 whole, which is shorter than its diff:
```python
import functools

import jax
import jax.numpy as jnp
from jax import lax
from jax.experimental import pallas as pl
from jax.experimental.pallas import tpu as pltpu
from jax.sharding import PartitionSpec as P

MESH = pl.DeviceIdType.MESH
time_step = 0.03
SIDE = 16
LANES = SIDE * SIDE


def moved(q, shift):
    return pltpu.roll(q, (-shift) % LANES, q.ndim - 1)


def update(q, behind, ahead, load, s):
    spread = None
    for n, other in enumerate(
        (behind, ahead, moved(q, -SIDE), moved(q, SIDE), moved(q, -1), moved(q, 1))
    ):
        a, b = load(n)
        term = (s * a + b) * (other - q)
        spread = term if spread is None else spread + term
    return q + spread


def weights(k, k_behind, k_ahead, u, v, w, store):
    lane = lax.broadcasted_iota(jnp.int32, k.shape, k.ndim - 1)
    y, z = lane // SIDE, lane % SIDE
    sides = (
        (k_behind, u, False, None),
        (k_ahead, u, True, None),
        (moved(k, -SIDE), v, False, y > 0),
        (moved(k, SIDE), v, True, y < SIDE - 1),
        (moved(k, -1), w, False, z > 0),
        (moved(k, 1), w, True, z < SIDE - 1),
    )
    for n, (other, speed, up, inside) in enumerate(sides):
        a = (0.5 * time_step) * (k + other)
        b = (-time_step) * jnp.minimum(speed, 0.0) if up else time_step * jnp.maximum(speed, 0.0)
        if inside is not None:
            a, b = jnp.where(inside, a, 0.0), jnp.where(inside, b, 0.0)
        store(n, a, b)


def joined(q, first, last):
    rows = q.shape[0]
    row = lax.broadcasted_iota(jnp.int32, q.shape, 0)
    behind = jnp.where(row == 0, jnp.broadcast_to(first, q.shape), pltpu.roll(q, 1, 0))
    ahead = jnp.where(row == rows - 1, jnp.broadcast_to(last, q.shape), pltpu.roll(q, rows - 1, 0))
    return behind, ahead


def step_kernel(fields, boxes, scale, state, kappa, flow, res, up, down, low, high, wm, we, edge, send, recv):
    xs, bx, count = lax.axis_index("xs"), lax.axis_index("bx"), lax.axis_size("xs")
    after, before = (lax.rem(xs + 1, count), bx), (lax.rem(xs + count - 1, count), bx)
    barrier = pltpu.get_barrier_semaphore()
    for peer in (after, before):
        pl.semaphore_signal(barrier, inc=1, device_id=peer, device_id_type=MESH)

    far_k, near_k, near_v = 2 * fields, 2 * fields + 1, 2 * fields + 2
    for b in range(boxes):
        one = pl.ds(b, 1)
        for buf, far, near in ((up, SIDE - 2, SIDE - 1), (down, 1, 0)):

            @pl.loop(0, fields)
            def _(f, buf=buf, far=far, near=near, b=b, one=one):
                buf[f, one, :] = state[b, f, pl.ds(far, 1), :]
                buf[fields + f, one, :] = state[b, f, pl.ds(near, 1), :]

            buf[far_k, one, :] = kappa[b, pl.ds(far, 1), :]
            buf[near_k, one, :] = kappa[b, pl.ds(near, 1), :]
            for d in range(3):
                buf[near_v + d, one, :] = flow[b, d, pl.ds(near, 1), :]

    pl.semaphore_wait(barrier, 2)
    copies = [
        pltpu.make_async_remote_copy(
            src_ref=src, dst_ref=dst, send_sem=send.at[i], recv_sem=recv.at[i], device_id=peer, device_id_type=MESH
        )
        for i, (src, dst, peer) in enumerate(((up, low, after), (down, high, before)))
    ]
    for copy in copies:
        copy.start()
    for copy in copies:
        copy.wait()

    def keep(ref, at):
        def store(n, a, b):
            ref[(0, n) + at] = a
            ref[(1, n) + at] = b

        return store

    for i, (far, near, own) in enumerate(((low, low, down), (high, high, up))):
        ends = (far[far_k], own[near_k])
        weights(near[near_k], *(ends if i == 0 else ends[::-1]), *(near[near_v + d] for d in range(3)), keep(we, (i,)))
    for b in range(boxes):
        k = kappa[b]
        behind, ahead = joined(k, low[near_k, pl.ds(b, 1), :], high[near_k, pl.ds(b, 1), :])
        weights(k, behind, ahead, flow[b, 0], flow[b, 1], flow[b, 2], keep(wm, (b,)))

    @pl.loop(0, fields)
    def _(f):
        s = scale[f]
        for i, (halo, own) in enumerate(((low, down), (high, up))):
            ends = (halo[f], own[fields + f])
            edge[i] = update(
                halo[fields + f], *(ends if i == 0 else ends[::-1]), lambda n: (we[0, n, i], we[1, n, i]), s
            )
        for b in range(boxes):
            load = lambda n: (wm[0, n, b], wm[1, n, b])
            one = pl.ds(b, 1)
            q = state[b, f]
            q = update(q, *joined(q, low[fields + f, one, :], high[fields + f, one, :]), load, s)
            res[f, b] = update(q, *joined(q, edge[0, one, :], edge[1, one, :]), load, s)


def two_steps(state, kappa, flow, scale):
    boxes, fields = state.shape[:2]
    halo = pltpu.VMEM((2 * fields + 5, boxes, LANES), jnp.float32)
    vmem = pl.BlockSpec(memory_space=pltpu.VMEM)
    return pl.pallas_call(
        functools.partial(step_kernel, fields, boxes),
        out_shape=jax.ShapeDtypeStruct((fields, boxes, SIDE, LANES), jnp.float32),
        in_specs=[pl.BlockSpec(memory_space=pltpu.SMEM), vmem, vmem, vmem],
        out_specs=vmem,
        scratch_shapes=[
            halo,
            halo,
            halo,
            halo,
            pltpu.VMEM((2, 6, boxes, SIDE, LANES), jnp.float32),
            pltpu.VMEM((2, 6, 2, boxes, LANES), jnp.float32),
            pltpu.VMEM((2, boxes, LANES), jnp.float32),
            pltpu.SemaphoreType.DMA((2,)),
            pltpu.SemaphoreType.DMA((2,)),
        ],
        compiler_params=pltpu.CompilerParams(collective_id=0, has_side_effects=True, vmem_limit_bytes=40 << 20),
        name="two_steps",
    )(scale, state, kappa, flow)


def on_device(state, diffusivity, velocity, species_scale, new_owner):
    owners = lax.axis_size("bx")
    here = lax.axis_index("bx")
    holding = state.shape[1]
    local_owner = lax.dynamic_slice_in_dim(new_owner, here * holding, holding)
    moving = local_owner != here
    targets = jnp.arange(owners, dtype=jnp.int32)
    picked = (local_owner[None, :] == targets[:, None]) & moving[None, :]
    source_slot = jnp.sum(jnp.where(picked, jnp.arange(holding, dtype=jnp.int32)[None, :], 0), axis=1)
    present = jnp.any(picked, axis=1)
    staying = jnp.logical_not(moving).reshape(holding, 1, 1, 1)
    result = jnp.swapaxes(two_steps(state[0], diffusivity[0], velocity[0], species_scale), 0, 1)
    chosen = jnp.stack([lax.dynamic_index_in_dim(result, source_slot[o], 0, keepdims=False) for o in range(owners)])
    arrived = lax.all_to_all(
        jnp.where(present.reshape(owners, 1, 1, 1), chosen, 0.0), "bx", split_axis=0, concat_axis=0, tiled=True
    )
    return jnp.concatenate([jnp.where(staying, result, 0.0), arrived], axis=0)[None]


def solution(mesh):
    in_specs = (
        P("xs", "bx", None, None, None),
        P("xs", "bx", None, None),
        P("xs", "bx", None, None, None),
        P(),
        P(),
    )
    out_specs = P("xs", "bx", None, None, None)
    return jax.shard_map(on_device, mesh=mesh, in_specs=in_specs, out_specs=out_specs, check_vma=False)
```

time: 317 us -> 190 us (0.60)
  the two profiles are of different devices: /device:TPU:6 before, /device:TPU:1 now
where the time goes in v1:
time: 190 us; the launch traced here: 189 us
  blocking collectives  93.7 us (49%)
  between operations  60.7 us (32%)
  Pallas kernels  21.7 us (11%)
  other arithmetic  6.75 us (4%)
  local copies, waits for them, and re-layouts  6.29 us (3%)
    all_to_all x1, blocking collectives, on_device(): lax.all_to_all(jnp.where(present.reshape(owners, 1, 1, 1), chosen, 0.0),...  93.7 us
    pallas_call x1, Pallas kernels, two_steps(): pl.pallas_call(functools.partial(step_kernel, fields, boxes), out_shape=j...  21.7 us
    broadcast_in_dim x1, other arithmetic, on_device(): jnp.concatenate([jnp.where(staying, result, 0.0), arrived], axis=0)[None]  4.83 us
    unnamed x39, local copies, waits for them, and re-layouts  4.81 us

profile of v1, /device:TPU:1, one launch (start us, length us, event | category | flops | bytes accessed | tf_op | source)
XLA Modules:
  0.0 189.2 jit_solution(3799679243136985114)
XLA Ops:
  0.0 0.8 fusion.2
  0.8 0.1 select_reduce_fusion
  0.8 0.1 fusion.1
  0.9 0.7 fusion.4
  17.9 0.7 fusion.3
  62.8 0.0 copy-start
  62.8 1.5 copy-done
  64.3 0.0 copy-start.1
  64.3 1.0 copy-done.1
  65.3 0.0 copy-start.2
  65.3 0.9 copy-done.2
  66.2 0.0 copy-start.3
  66.2 0.7 copy-done.3
  66.8 21.7 %two_steps.1 = f32[14,8,16,256]{3,2,1,0:T(8,128)S(1)} custom-call(f32[14]{0:T(128)S(1)} %copy-done.3, f32[8,14,16,256]{3,2,1,0:T(8,128)S(1)} %bitcast.105, f32[8,16,256]{2,1,0:T(8,128)S(1)} %bitcast.107, f32[8,3,16,256]{3,2,1,0:T(8,128)S(1)} %bitcast.106), custom_call_target="tpu_custom_call" | custom-call | tf_op jit(solution)/shard_map/two_steps/pallas_call | solution.py:127
  89.6 1.0 broadcast_select_fusion
  90.6 93.7 %all_to_all.5 = f32[32,14,16,256]{3,2,1,0:T(8,128)S(1)} all-to-all(f32[32,14,16,256]{3,2,1,0:T(8,128)S(1)} %broadcast_select_fusion), channel_id=1, replica_groups=mesh['xs'=4,'bx'=32] {'bx'}, dimensions={0} | all-to-all | bytes 14680064 | tf_op jit(solution)/shard_map/all_to_all | solution.py:161
  184.3 4.8 %maximum_bitcast_fusion = f32[1,40,14,16,256]{4,3,2,1,0:T(8,128)} fusion(f32[32,14,16,256]{3,2,1,0:T(8,128)S(1)} %all_to_all.5, f32[14,8,16,256]{3,2,1,0:T(8,128)S(1)} %two_steps.1, pred[8]{0:T(512)(128)(4,1)S(1)} %get-tuple-element.5), kind=kLoop, calls=%fused_computation | loop fusion | flops 2752512 | bytes 18350088 | tf_op jit(solution)/shard_map/broadcast_in_dim | solution.py:164
  (32 shorter events, 0.8 us)
Async XLA Ops:
  62.8 1.5 copy-start
  64.3 1.0 copy-start.1
  65.3 0.9 copy-start.2
  66.2 0.7 copy-start.3

commit v2 on v1

--- a/solution.py
+++ b/solution.py
@@ -55,12 +55,147 @@
     return behind, ahead
 
 
-def step_kernel(fields, boxes, scale, state, kappa, flow, res, up, down, low, high, wm, we, edge, send, recv):
-    xs, bx, count = lax.axis_index("xs"), lax.axis_index("bx"), lax.axis_size("xs")
-    after, before = (lax.rem(xs + 1, count), bx), (lax.rem(xs + count - 1, count), bx)
+I32 = jnp.int32
+CAPS = (7, 6, 11, 8)
+RING = 4
+TABLE = 256
+FINAL = 128
+
+
+def count(mask):
+    return jnp.sum(jnp.where(mask, 1, 0), axis=0, keepdims=True)
+
+
+def column(row):
+    n = row.shape[1]
+    eye = lax.broadcasted_iota(I32, (n, n), 0) == lax.broadcasted_iota(I32, (n, n), 1)
+    return jnp.sum(jnp.where(eye, row, 0), axis=1, keepdims=True)
+
+
+def hops(at, d, node_up, node_down, first, second):
+    n = at.shape[1]
+    earlier = lax.broadcasted_iota(I32, (n, n), 0) < lax.broadcasted_iota(I32, (n, n), 1)
+    at_c, d_c = column(at), column(d)
+    here = at_c == at
+    n1, n2, n3 = (count(here & (d_c == k)) for k in (1, 2, 3))
+    r = count(here & (d_c == d) & earlier)
+    half = jnp.clip((n2 + n3 - n1 + 1) >> 1, 0, n2)
+    two = d == 2
+    up = jnp.where(two, jnp.where(r < half, 1, 0), jnp.where(d == 1, 1, 0))
+    rank = jnp.where(two, jnp.where(r < half, r, r - half), jnp.where(d == 1, half + r, n2 - half + r))
+    mid = jnp.where(up == 1, node_up, node_down)
+    local = count((at_c == mid) & (column(up) == up) & (d_c > 0))
+    late = rank >= first
+    slot = jnp.where(two, jnp.maximum(local - first, 0) + rank, rank - first)
+    lost = (two & (late | (slot >= second))) | ((d > 0) & jnp.logical_not(two) & (slot >= second))
+    return up, rank, late, slot, mid, jnp.sum(jnp.where(lost, 1, 0), keepdims=True)
+
+
+def plan(owner, z, y, net):
+    n = owner.shape[1]
+    ka, kb, kc, kd = CAPS
+    b = lax.broadcasted_iota(I32, owner.shape, 1)
+    home = b // 8
+    moving = owner != home
+
+    def pq(chip):
+        return (chip % RING, chip // RING) if net == 0 else (chip // RING, chip % RING)
+
+    node = lambda p, q: p * RING + q
+    p0, q0 = pq(home // 2)
+    p1, q1 = pq(jnp.where(moving, owner, home) // 2)
+    me = node(y, z) if net == 0 else node(z, y)
+    turn = lambda p, k: (p + k) % RING
+    base_a = 16
+    base_b = base_a + 2 * ka
+    base_c = base_b + 2 * kb
+    base_d = base_c + 2 * kc
+    own = b % 16
+    d1 = turn(p1 - p0, RING)
+    up1, rank1, late1, slot1, mid1, lost1 = hops(
+        node(p0, q0), d1, node(turn(p0, 1), q0), node(turn(p0, 3), q0), ka, kb
+    )
+    in_a = base_a + (1 - up1) * ka + rank1
+    at1 = jnp.where(d1 == 0, own, jnp.where((d1 == 2) | late1, base_b + (1 - up1) * kb + slot1, in_a))
+    d2 = turn(q1 - q0, RING)
+    up2, rank2, late2, slot2, mid2, lost2 = hops(
+        node(p1, q0), d2, node(p1, turn(q0, 1)), node(p1, turn(q0, 3)), kc, kd
+    )
+    in_c = base_c + (1 - up2) * kc + rank2
+    at2 = jnp.where(d2 == 0, at1, jnp.where((d2 == 2) | late2, base_d + (1 - up2) * kd + slot2, in_c))
+    nodes = (node(p0, q0), node(p1, q0), node(p1, q1))
+    entries = (
+        ((nodes[0] == me) & (d1 > 0) & jnp.logical_not(late1), (1 - up1) * ka + rank1, own),
+        ((nodes[0] == me) & (d1 > 0) & (d1 != 2) & late1, 2 * ka + (1 - up1) * kb + slot1, own),
+        ((mid1 == me) & (d1 == 2), 2 * ka + (1 - up1) * kb + slot1, in_a),
+        ((nodes[1] == me) & (d2 > 0) & jnp.logical_not(late2), 2 * (ka + kb) + (1 - up2) * kc + rank2, at1),
+        ((nodes[1] == me) & (d2 > 0) & (d2 != 2) & late2, 2 * (ka + kb + kc) + (1 - up2) * kd + slot2, at1),
+        ((mid2 == me) & (d2 == 2), 2 * (ka + kb + kc) + (1 - up2) * kd + slot2, in_c),
+        ((nodes[2] == me) & moving, FINAL + (owner % 2) * 32 + home, at2 + 1),
+    )
+    lane = lax.broadcasted_iota(I32, (n, TABLE), 1)
+    table = jnp.where(lax.broadcasted_iota(I32, (1, TABLE), 1) >= FINAL, -1, 0)
+    for mask, slot, place in entries:
+        slot, place = column(jnp.where(mask, slot, -1)), column(place)
+        table = table + jnp.sum(jnp.where(lane == slot, place, 0), axis=0, keepdims=True)
+    top = 16 + 2 * sum(CAPS) - 1
+    return jnp.clip(table, -1, top), lost1 + lost2
+
+
+def plan_kernel(owner, table):
+    bx = lax.axis_index("bx")
+    chip, core = bx // 2, bx % 2
+    z, y = chip // RING, chip % RING
+    one, lost_one = plan(owner[...], z, y, 0)
+    two, lost_two = plan(owner[...], z, y, 1)
+    lost = lost_one + lost_two
+    row = jnp.where(core == 0, one, two)
+    lane = lax.broadcasted_iota(I32, row.shape, 1)
+    table[...] = jnp.where(lane == TABLE - 1, jnp.broadcast_to(lost, row.shape), row)
+
+
+def make_plan(new_owner):
+    vmem = pl.BlockSpec(memory_space=pltpu.VMEM)
+    return pl.pallas_call(
+        plan_kernel,
+        out_shape=jax.ShapeDtypeStruct((1, TABLE), I32),
+        in_specs=[vmem],
+        out_specs=vmem,
+        name="plan",
+    )(new_owner.reshape(1, -1))
+
+
+def regrid_kernel(
+    fields, boxes, homes, table, owner, scale, state_hbm, kappa_hbm, flow_hbm, res, stay, near_out, far_out,
+    state, kappa, flow, up, down, low, high, wm, we, edge, sib, pool, fin, sa, sb, sc, sd, ra, rb, rc, rd,
+    in_sem, halo_sem, sib_sem, fin_sem, send, recv,
+):
+    xs, bx, n_xs = lax.axis_index("xs"), lax.axis_index("bx"), lax.axis_size("xs")
+    chip, core = bx // 2, bx % 2
+    z, y = chip // RING, chip % RING
+    half = fields // 2
+
+    def device(dz, dy):
+        return (xs, (((z + dz) % RING) * RING + (y + dy) % RING) * 2 + core)
+
+    def peer(ring, step):
+        along_y = (1 - core) if ring == 0 else core
+        return device(step * (1 - along_y), step * along_y)
+
+    sibling = (xs, bx + 1 - 2 * core)
+    after, before = (lax.rem(xs + 1, n_xs), bx), (lax.rem(xs + n_xs - 1, n_xs), bx)
+    around = [peer(ring, step) for ring in (0, 1) for step in (1, RING - 1)]
     barrier = pltpu.get_barrier_semaphore()
-    for peer in (after, before):
-        pl.semaphore_signal(barrier, inc=1, device_id=peer, device_id_type=MESH)
+    for other in (after, before, sibling, *around):
+        pl.semaphore_signal(barrier, inc=1, device_id=other, device_id_type=MESH)
+    loads = [
+        pltpu.make_async_copy(src, dst, in_sem.at[i])
+        for i, (src, dst) in enumerate(((state_hbm, state), (kappa_hbm, kappa), (flow_hbm, flow)))
+    ]
+    for copy in loads:
+        copy.start()
+    for copy in loads:
+        copy.wait()
 
     far_k, near_k, near_v = 2 * fields, 2 * fields + 1, 2 * fields + 2
     for b in range(boxes):
@@ -77,12 +212,17 @@
             for d in range(3):
                 buf[near_v + d, one, :] = flow[b, d, pl.ds(near, 1), :]
 
-    pl.semaphore_wait(barrier, 2)
+    pl.semaphore_wait(barrier, 3 + len(around))
     copies = [
         pltpu.make_async_remote_copy(
-            src_ref=src, dst_ref=dst, send_sem=send.at[i], recv_sem=recv.at[i], device_id=peer, device_id_type=MESH
+            src_ref=src,
+            dst_ref=dst,
+            send_sem=halo_sem.at[0, i],
+            recv_sem=halo_sem.at[1, i],
+            device_id=other,
+            device_id_type=MESH,
         )
-        for i, (src, dst, peer) in enumerate(((up, low, after), (down, high, before)))
+        for i, (src, dst, other) in enumerate(((up, low, after), (down, high, before)))
     ]
     for copy in copies:
         copy.start()
@@ -104,8 +244,7 @@
         behind, ahead = joined(k, low[near_k, pl.ds(b, 1), :], high[near_k, pl.ds(b, 1), :])
         weights(k, behind, ahead, flow[b, 0], flow[b, 1], flow[b, 2], keep(wm, (b,)))
 
-    @pl.loop(0, fields)
-    def _(f):
+    def advance(f):
         s = scale[f]
         for i, (halo, own) in enumerate(((low, down), (high, up))):
             ends = (halo[f], own[fields + f])
@@ -117,51 +256,210 @@
             one = pl.ds(b, 1)
             q = state[b, f]
             q = update(q, *joined(q, low[fields + f, one, :], high[fields + f, one, :]), load, s)
-            res[f, b] = update(q, *joined(q, edge[0, one, :], edge[1, one, :]), load, s)
-
-
-def two_steps(state, kappa, flow, scale):
+            q = update(q, *joined(q, edge[0, one, :], edge[1, one, :]), load, s)
+            res[f, b] = q
+            stay[f, b] = jnp.where(owner[bx * boxes + b] == bx, q, 0.0)
+
+    def to_sibling(t):
+        return pltpu.make_async_remote_copy(
+            src_ref=res.at[(1 - core) * half + t],
+            dst_ref=sib.at[t],
+            send_sem=sib_sem.at[0, t],
+            recv_sem=sib_sem.at[1, t],
+            device_id=sibling,
+            device_id_type=MESH,
+        )
+
+    def back(t):
+        return pltpu.make_async_remote_copy(
+            src_ref=fin.at[t],
+            dst_ref=far_out.at[t],
+            send_sem=fin_sem.at[0, t],
+            recv_sem=fin_sem.at[1, t],
+            device_id=sibling,
+            device_id_type=MESH,
+        )
+
+    outgoing, incoming = (sa, sb, sc, sd), (ra, rb, rc, rd)
+    start = [2 * sum(CAPS[:i]) for i in range(4)]
+
+    def hop(stage, way, t):
+        return pltpu.make_async_remote_copy(
+            src_ref=outgoing[stage].at[t, way],
+            dst_ref=incoming[stage].at[t, way],
+            send_sem=send.at[stage, way, t],
+            recv_sem=recv.at[stage, way, t],
+            device_id=around[(stage // 2) * 2 + way],
+            device_id_type=MESH,
+        )
+
+    def compute(t):
+        @pl.loop(0, 2)
+        def _(i):
+            advance(i * half + t)
+
+        to_sibling(t).start()
+
+    def gather(stage, t):
+        for way in (0, 1):
+            for k in range(CAPS[stage]):
+                outgoing[stage][t, way, k] = pool[t, table[0, start[stage] + way * CAPS[stage] + k]]
+            hop(stage, way, t).start()
+
+    def take(stage, t):
+        for way in (0, 1):
+            hop(stage, way, t).wait_recv()
+            pool[t, pl.ds(16 + start[stage] + way * CAPS[stage], CAPS[stage])] = incoming[stage][t, way]
+
+    def first(t):
+        to_sibling(t).wait_recv()
+        pool[t, pl.ds(core * boxes, boxes)] = res[core * half + t]
+        pool[t, pl.ds((1 - core) * boxes, boxes)] = sib[t]
+        gather(0, t)
+
+    def middle(stage):
+        def run(t):
+            take(stage - 1, t)
+            gather(stage, t)
+
+        return run
+
+    def last(t):
+        take(3, t)
+        for dst, whose in ((fin, 1 - core), (near_out, core)):
+
+            @pl.loop(0, homes)
+            def _(h, dst=dst, whose=whose):
+                place = table[0, FINAL + whose * 32 + h]
+                dst[t, h] = jnp.where(place >= 0, pool[t, jnp.maximum(place, 0)], 0.0)
+
+            if dst is fin:
+                back(t).start()
+
+    steps = (first, middle(1), middle(2), middle(3), last)
+    compute(0)
+
+    @pl.loop(0, half + len(steps) - 1)
+    def _(t):
+        for lag, run in enumerate(steps):
+
+            @pl.when((t >= lag) & (t < half + lag))
+            def _(run=run, lag=lag):
+                run(t - lag)
+
+        @pl.when(t + 1 < half)
+        def _():
+            compute(t + 1)
+
+    @pl.loop(0, half)
+    def _(t):
+        to_sibling(t).wait_send()
+        back(t).wait()
+        for stage in range(4):
+            for way in (0, 1):
+                hop(stage, way, t).wait_send()
+
+
+def regrid(table, new_owner, scale, state, kappa, flow):
     boxes, fields = state.shape[:2]
-    halo = pltpu.VMEM((2 * fields + 5, boxes, LANES), jnp.float32)
-    vmem = pl.BlockSpec(memory_space=pltpu.VMEM)
+    homes = new_owner.shape[0] // boxes
+    half = fields // 2
+    f32 = jnp.float32
+    vmem, smem, hbm = (pl.BlockSpec(memory_space=m) for m in (pltpu.VMEM, pltpu.SMEM, pltpu.HBM))
+    box = (SIDE, LANES)
+    halo = pltpu.VMEM((2 * fields + 5, boxes, LANES), f32)
+    slots = [pltpu.VMEM((half, 2, k) + box, f32) for k in CAPS]
+    dma = pltpu.SemaphoreType.DMA
     return pl.pallas_call(
-        functools.partial(step_kernel, fields, boxes),
-        out_shape=jax.ShapeDtypeStruct((fields, boxes, SIDE, LANES), jnp.float32),
-        in_specs=[pl.BlockSpec(memory_space=pltpu.SMEM), vmem, vmem, vmem],
-        out_specs=vmem,
+        functools.partial(regrid_kernel, fields, boxes, homes),
+        out_shape=[jax.ShapeDtypeStruct((fields, boxes) + box, f32)] * 2
+        + [jax.ShapeDtypeStruct((half, homes) + box, f32)] * 2,
+        in_specs=[smem, smem, smem, hbm, hbm, hbm],
+        out_specs=[vmem] * 4,
         scratch_shapes=[
+            pltpu.VMEM((boxes, fields) + box, f32),
+            pltpu.VMEM((boxes,) + box, f32),
+            pltpu.VMEM((boxes, 3) + box, f32),
             halo,
             halo,
             halo,
             halo,
-            pltpu.VMEM((2, 6, boxes, SIDE, LANES), jnp.float32),
-            pltpu.VMEM((2, 6, 2, boxes, LANES), jnp.float32),
-            pltpu.VMEM((2, boxes, LANES), jnp.float32),
-            pltpu.SemaphoreType.DMA((2,)),
-            pltpu.SemaphoreType.DMA((2,)),
+            pltpu.VMEM((2, 6, boxes) + box, f32),
+            pltpu.VMEM((2, 6, 2, boxes, LANES), f32),
+            pltpu.VMEM((2, boxes, LANES), f32),
+            pltpu.VMEM((half, boxes) + box, f32),
+            pltpu.VMEM((half, 16 + 2 * sum(CAPS)) + box, f32),
+            pltpu.VMEM((half, homes) + box, f32),
+            *slots,
+            *slots,
+            dma((3,)),
+            dma((2, 2)),
+            dma((2, half)),
+            dma((2, half)),
+            dma((4, 2, half)),
+            dma((4, 2, half)),
         ],
-        compiler_params=pltpu.CompilerParams(collective_id=0, has_side_effects=True, vmem_limit_bytes=40 << 20),
-        name="two_steps",
-    )(scale, state, kappa, flow)
-
-
-def on_device(state, diffusivity, velocity, species_scale, new_owner):
-    owners = lax.axis_size("bx")
-    here = lax.axis_index("bx")
-    holding = state.shape[1]
+        compiler_params=pltpu.CompilerParams(collective_id=0, has_side_effects=True, vmem_limit_bytes=48 << 20),
+        name="regrid",
+    )(table, new_owner, scale, state, kappa, flow)
+
+
+def place_kernel(stay, near, far, out):
+    core = lax.axis_index("bx") % 2
+    boxes = stay.shape[2]
+    for b in range(boxes):
+        for group in (0, 1):
+            out[b, group, 0] = stay[group, 0, b]
+    out[boxes:, core, 0] = near[0]
+    out[boxes:, 1 - core, 0] = far[0]
+
+
+def placed(stay, near, far):
+    fields, boxes = stay.shape[:2]
+    half, homes = near.shape[:2]
+    box = stay.shape[2:]
+    arrived = pl.BlockSpec((1, homes) + box, lambda t: (t, 0, 0, 0))
+    out = pl.pallas_call(
+        place_kernel,
+        grid=(half,),
+        out_shape=jax.ShapeDtypeStruct((boxes + homes, 2, half) + box, stay.dtype),
+        in_specs=[pl.BlockSpec((2, 1, boxes) + box, lambda t: (0, t, 0, 0, 0)), arrived, arrived],
+        out_specs=pl.BlockSpec((boxes + homes, 2, 1) + box, lambda t: (0, 0, t, 0, 0)),
+        compiler_params=pltpu.CompilerParams(vmem_limit_bytes=16 << 20),
+        name="placed",
+    )(stay.reshape((2, half, boxes) + box), near, far)
+    return out.reshape((boxes + homes, fields) + box)
+
+
+def dense(result, new_owner):
+    owners, here = lax.axis_size("bx"), lax.axis_index("bx")
+    holding = result.shape[1]
     local_owner = lax.dynamic_slice_in_dim(new_owner, here * holding, holding)
     moving = local_owner != here
-    targets = jnp.arange(owners, dtype=jnp.int32)
+    targets = jnp.arange(owners, dtype=I32)
     picked = (local_owner[None, :] == targets[:, None]) & moving[None, :]
-    source_slot = jnp.sum(jnp.where(picked, jnp.arange(holding, dtype=jnp.int32)[None, :], 0), axis=1)
-    present = jnp.any(picked, axis=1)
+    source = jnp.sum(jnp.where(picked, jnp.arange(holding, dtype=I32)[None, :], 0), axis=1)
+    present = jnp.any(picked, axis=1).reshape(owners, 1, 1, 1)
+    result = jnp.swapaxes(result, 0, 1)
+    chosen = lax.map(lambda i: lax.dynamic_index_in_dim(result, i, 0, keepdims=False), source)
+    arrived = lax.all_to_all(jnp.where(present, chosen, 0.0), "bx", split_axis=0, concat_axis=0, tiled=True)
     staying = jnp.logical_not(moving).reshape(holding, 1, 1, 1)
-    result = jnp.swapaxes(two_steps(state[0], diffusivity[0], velocity[0], species_scale), 0, 1)
-    chosen = jnp.stack([lax.dynamic_index_in_dim(result, source_slot[o], 0, keepdims=False) for o in range(owners)])
-    arrived = lax.all_to_all(
-        jnp.where(present.reshape(owners, 1, 1, 1), chosen, 0.0), "bx", split_axis=0, concat_axis=0, tiled=True
-    )
-    return jnp.concatenate([jnp.where(staying, result, 0.0), arrived], axis=0)[None]
+    return jnp.concatenate([jnp.where(staying, result, 0.0), arrived], axis=0)
+
+
+def on_device(state, diffusivity, velocity, species_scale, new_owner):
+    table = make_plan(new_owner)
+    res, stay, near, far = regrid(table, new_owner, species_scale, state[0], diffusivity[0], velocity[0])
+    result = lax.cond(
+        table[0, TABLE - 1] == 0,
+        lambda res, stay, near, far: placed(stay, near, far),
+        lambda res, stay, near, far: dense(res, new_owner),
+        res,
+        stay,
+        near,
+        far,
+    )
+    return result[None]
 
 
 def solution(mesh):

time: 190 us -> 97.8 us (0.51)
  blocking collectives: 93.7 us -> 0 us
  Pallas kernels: 21.7 us -> 87.7 us
  between operations: 60.7 us -> 0.68 us
  other arithmetic: 6.75 us -> 0 us
  local copies, waits for them, and re-layouts: 6.29 us -> 8.96 us
    all_to_all x1 -> x0, blocking collectives: 93.7 us -> none  [on_device(): lax.all_to_all(jnp.where(present.reshape(owners, 1, 1, 1), chosen, 0.0),...]
    pallas_call x1 -> x3, Pallas kernels: 21.7 us -> 87.7 us  [the longest x1 77 us: regrid(): pl.pallas_call(functools.partial(regrid_kernel, fields, boxes, homes), ou...]
    broadcast_in_dim x1 -> x0, other arithmetic: 4.83 us -> none  [on_device(): jnp.concatenate([jnp.where(staying, result, 0.0), arrived], axis=0)[None]]
    unnamed x39 -> x12, local copies, waits for them, and re-layouts: 4.81 us -> 8.38 us
where the time goes in v2:
time: 97.8 us; the launch traced here: 97.4 us
  Pallas kernels  87.7 us (90%)
  local copies, waits for them, and re-layouts  8.96 us (9%)
    pallas_call x1, Pallas kernels, regrid(): pl.pallas_call(functools.partial(regrid_kernel, fields, boxes, homes), ou...  77 us
    unnamed x12, local copies, waits for them, and re-layouts  8.38 us
    pallas_call x1, Pallas kernels, placed(): pl.pallas_call(place_kernel, grid=(half,), out_shape=jax.ShapeDtypeStruct...  6.05 us
    pallas_call x1, Pallas kernels, make_plan(): pl.pallas_call(plan_kernel, out_shape=jax.ShapeDtypeStruct((1, TABLE), I3...  4.64 us

profile of v2, /device:TPU:1, one launch (start us, length us, event | category | flops | bytes accessed | tf_op | source)
XLA Modules:
  0.0 97.4 jit_solution(3181160013911559826)
XLA Ops:
  0.0 4.6 %plan.1.table = s32[1,256]{1,0:T(1,128)} custom-call(s32[1,256]{1,0:T(1,128)} %bitcast.24), custom_call_target="tpu_custom_call" | custom-call | tf_op jit(solution)/shard_map/plan/pallas_call | solution.py:159
  4.6 0.0 copy-start
  4.6 1.5 %copy-done = f32[1,8,14,16,256]{4,3,2,1,0:T(8,128)S(1)} copy-done((f32[1,8,14,16,256]{4,3,2,1,0:T(8,128)S(1)}, f32[1,8,14,16,256]{4,3,2,1,0:T(8,128)}, u32[]{:S(2)}) %copy-start) | copy-done | bytes 1835032
  6.1 0.0 copy-start.1
  6.1 1.0 %copy-done.1 = f32[1,8,3,16,256]{4,3,2,1,0:T(8,128)S(1)} copy-done((f32[1,8,3,16,256]{4,3,2,1,0:T(8,128)S(1)}, f32[1,8,3,16,256]{4,3,2,1,0:T(8,128)}, u32[]{:S(2)}) %copy-start.1) | copy-done | bytes 393240
  7.1 0.0 copy-start.2
  7.1 0.9 copy-done.2
  8.0 0.0 copy-start.3
  8.0 0.7 copy-done.3
  8.7 0.0 copy-start.4
  8.7 0.7 copy-done.4
  9.4 77.0 %regrid.1 = (f32[14,8,16,256]{3,2,1,0:T(8,128)S(1)}, f32[14,8,16,256]{3,2,1,0:T(8,128)}, f32[7,32,16,256]{3,2,1,0:T(8,128)}, f32[7,32,16,256]{3,2,1,0:T(8,128)}) custom-call(s32[1,256]{1,0:T(1,128)S(1)} %copy-done.3, s32[256]{0:T(256)} %owner.1, f32[14]{0:T(128)S(1)} %copy-done.4, f32[8,14,16,256]{3,2,1,0:T(8,128)S(1)} %bitcast.18, ...), custom_call_target="tpu_custom_call" | custom-call | tf_op jit(solution)/shard_map/regrid/pallas_call | solution.py:373
  86.4 0.6 slice.4
  87.7 6.1 %conditional.1 = (f32[1,40,14,16,256]{4,3,2,1,0:T(8,128)S(1)}) conditional(s32[]{:T(128)} %bitcast.6, (s32[256]{0:T(256)}, f32[14,8,16,256]{3,2,1,0:T(8,128)S(1)}) %tuple.17, (f32[14,8,16,256]{3,2,1,0:T(8,128)}, f32[7,32,16,256]{3,2,1,0:T(8,128)}, f32[7,32,16,256]{3,2,1,0:T(8,128)}) %tuple.18), branch_computations={%region_0.5_spmd, %region_5.6_spmd} | conditional | flops 4589275 | bytes 70190216 | solution.py:453
  87.7 6.0 %placed.1 = f32[40,2,7,16,256]{4,3,2,1,0:T(8,128)S(1)} custom-call(f32[2,7,8,16,256]{4,3,2,1,0:T(8,128)} %bitcast.23, f32[7,32,16,256]{3,2,1,0:T(8,128)} %get-tuple-element.44.near, f32[7,32,16,256]{3,2,1,0:T(8,128)} %get-tuple-element.45.far), custom_call_target="tpu_custom_call" | custom-call | tf_op jit(solution)/shard_map/cond/branch_1_fun/placed/pallas_call | solution.py:422
  93.7 0.0 copy-start.5
  93.7 3.6 %copy-done.5 = f32[1,40,14,16,256]{4,3,2,1,0:T(8,128)} copy-done((f32[1,40,14,16,256]{4,3,2,1,0:T(8,128)}, f32[1,40,14,16,256]{4,3,2,1,0:T(8,128)S(1)}, u32[]{:S(2)}) %copy-start.5) | copy-done | bytes 9175064
Async XLA Ops:
  4.6 1.5 %copy-start = (f32[1,8,14,16,256]{4,3,2,1,0:T(8,128)S(1)}, f32[1,8,14,16,256]{4,3,2,1,0:T(8,128)}, u32[]{:S(2)}) copy-start(f32[1,8,14,16,256]{4,3,2,1,0:T(8,128)} %param.9) | copy-start | bytes 5505028
  6.1 1.0 %copy-start.1 = (f32[1,8,3,16,256]{4,3,2,1,0:T(8,128)S(1)}, f32[1,8,3,16,256]{4,3,2,1,0:T(8,128)}, u32[]{:S(2)}) copy-start(f32[1,8,3,16,256]{4,3,2,1,0:T(8,128)} %param.11) | copy-start | bytes 1179652
  7.1 0.9 copy-start.2
  8.0 0.7 copy-start.3
  8.7 0.7 copy-start.4
  93.7 3.7 %copy-start.5 = (f32[1,40,14,16,256]{4,3,2,1,0:T(8,128)}, f32[1,40,14,16,256]{4,3,2,1,0:T(8,128)S(1)}, u32[]{:S(2)}) copy-start(f32[1,40,14,16,256]{4,3,2,1,0:T(8,128)S(1)} %get-tuple-element.123) | copy-start | bytes 27525124

commit v3 on v2

--- a/solution.py
+++ b/solution.py
@@ -60,6 +60,7 @@
 RING = 4
 TABLE = 256
 FINAL = 128
+NONE = 16 + 2 * sum(CAPS)
 
 
 def count(mask):
@@ -131,44 +132,28 @@
         ((nodes[1] == me) & (d2 > 0) & jnp.logical_not(late2), 2 * (ka + kb) + (1 - up2) * kc + rank2, at1),
         ((nodes[1] == me) & (d2 > 0) & (d2 != 2) & late2, 2 * (ka + kb + kc) + (1 - up2) * kd + slot2, at1),
         ((mid2 == me) & (d2 == 2), 2 * (ka + kb + kc) + (1 - up2) * kd + slot2, in_c),
-        ((nodes[2] == me) & moving, FINAL + (owner % 2) * 32 + home, at2 + 1),
+        ((nodes[2] == me) & moving, FINAL + (owner % 2) * 32 + home, at2 - NONE),
     )
     lane = lax.broadcasted_iota(I32, (n, TABLE), 1)
-    table = jnp.where(lax.broadcasted_iota(I32, (1, TABLE), 1) >= FINAL, -1, 0)
+    table = jnp.where(lax.broadcasted_iota(I32, (1, TABLE), 1) >= FINAL, NONE, 0)
     for mask, slot, place in entries:
         slot, place = column(jnp.where(mask, slot, -1)), column(place)
         table = table + jnp.sum(jnp.where(lane == slot, place, 0), axis=0, keepdims=True)
-    top = 16 + 2 * sum(CAPS) - 1
-    return jnp.clip(table, -1, top), lost1 + lost2
-
-
-def plan_kernel(owner, table):
-    bx = lax.axis_index("bx")
-    chip, core = bx // 2, bx % 2
-    z, y = chip // RING, chip % RING
-    one, lost_one = plan(owner[...], z, y, 0)
-    two, lost_two = plan(owner[...], z, y, 1)
-    lost = lost_one + lost_two
+    return jnp.clip(table, 0, NONE), lost1 + lost2
+
+
+def both_plans(owner, z, y, core):
+    one, lost_one = plan(owner, z, y, 0)
+    two, lost_two = plan(owner, z, y, 1)
     row = jnp.where(core == 0, one, two)
     lane = lax.broadcasted_iota(I32, row.shape, 1)
-    table[...] = jnp.where(lane == TABLE - 1, jnp.broadcast_to(lost, row.shape), row)
-
-
-def make_plan(new_owner):
-    vmem = pl.BlockSpec(memory_space=pltpu.VMEM)
-    return pl.pallas_call(
-        plan_kernel,
-        out_shape=jax.ShapeDtypeStruct((1, TABLE), I32),
-        in_specs=[vmem],
-        out_specs=vmem,
-        name="plan",
-    )(new_owner.reshape(1, -1))
+    return jnp.where(lane == TABLE - 1, jnp.broadcast_to(jnp.minimum(lost_one + lost_two, 1), row.shape), row)
 
 
 def regrid_kernel(
-    fields, boxes, homes, table, owner, scale, state_hbm, kappa_hbm, flow_hbm, res, stay, near_out, far_out,
-    state, kappa, flow, up, down, low, high, wm, we, edge, sib, pool, fin, sa, sb, sc, sd, ra, rb, rc, rd,
-    in_sem, halo_sem, sib_sem, fin_sem, send, recv,
+    fields, boxes, homes, owner_row, owner, scale, state_hbm, kappa_hbm, flow_hbm, out, res_hbm, lost,
+    res, state, kappa, flow, up, down, low, high, wm, we, edge, sib, pool, fin, sa, sb, sc, sd, ra, rb, rc, rd,
+    row, table, in_sem, halo_sem, halo_sent, sib_sem, sib_sent, fin_sem, keep_sem, send, recv,
 ):
     xs, bx, n_xs = lax.axis_index("xs"), lax.axis_index("bx"), lax.axis_size("xs")
     chip, core = bx // 2, bx % 2
@@ -198,36 +183,49 @@
         copy.wait()
 
     far_k, near_k, near_v = 2 * fields, 2 * fields + 1, 2 * fields + 2
-    for b in range(boxes):
-        one = pl.ds(b, 1)
-        for buf, far, near in ((up, SIDE - 2, SIDE - 1), (down, 1, 0)):
-
-            @pl.loop(0, fields)
-            def _(f, buf=buf, far=far, near=near, b=b, one=one):
-                buf[f, one, :] = state[b, f, pl.ds(far, 1), :]
-                buf[fields + f, one, :] = state[b, f, pl.ds(near, 1), :]
-
+    for buf, far, near in ((up, SIDE - 2, SIDE - 1), (down, 1, 0)):
+        for b in range(boxes):
+            one = pl.ds(b, 1)
             buf[far_k, one, :] = kappa[b, pl.ds(far, 1), :]
             buf[near_k, one, :] = kappa[b, pl.ds(near, 1), :]
             for d in range(3):
                 buf[near_v + d, one, :] = flow[b, d, pl.ds(near, 1), :]
 
+        @pl.loop(0, half)
+        def _(t, buf=buf, far=far, near=near):
+            for i in (0, 1):
+                for side, row in enumerate((far, near)):
+                    rows = [state[b, i * half + t, pl.ds(row, 1), :] for b in range(boxes)]
+                    for b in range(boxes):
+                        buf[4 * t + 2 * i + side, pl.ds(b, 1), :] = rows[b]
+
     pl.semaphore_wait(barrier, 3 + len(around))
-    copies = [
-        pltpu.make_async_remote_copy(
-            src_ref=src,
-            dst_ref=dst,
-            send_sem=halo_sem.at[0, i],
-            recv_sem=halo_sem.at[1, i],
+
+    def ends_of(way, first, rows, part):
+        src, dst, other = ((up, low, after), (down, high, before))[way]
+        return pltpu.make_async_remote_copy(
+            src_ref=src.at[pl.ds(first, rows)],
+            dst_ref=dst.at[pl.ds(first, rows)],
+            send_sem=halo_sent.at[way],
+            recv_sem=halo_sem.at[way, part],
             device_id=other,
             device_id_type=MESH,
         )
-        for i, (src, dst, other) in enumerate(((up, low, after), (down, high, before)))
-    ]
-    for copy in copies:
+
+    coefficients = [ends_of(way, far_k, 5, half) for way in (0, 1)]
+    for copy in coefficients:
         copy.start()
-    for copy in copies:
-        copy.wait()
+
+    @pl.loop(0, half)
+    def _(t):
+        for way in (0, 1):
+            ends_of(way, 4 * t, 4, t).start()
+
+    row[...] = both_plans(owner_row[...], z, y, core)
+    to_scalars = pltpu.make_async_copy(row, table, in_sem.at[3])
+    to_scalars.start()
+    for copy in coefficients:
+        copy.wait_recv()
 
     def keep(ref, at):
         def store(n, a, b):
@@ -244,41 +242,37 @@
         behind, ahead = joined(k, low[near_k, pl.ds(b, 1), :], high[near_k, pl.ds(b, 1), :])
         weights(k, behind, ahead, flow[b, 0], flow[b, 1], flow[b, 2], keep(wm, (b,)))
 
-    def advance(f):
+    def advance(t, k):
+        f = k * half + t
         s = scale[f]
+        far, near = 4 * t + 2 * k, 4 * t + 2 * k + 1
         for i, (halo, own) in enumerate(((low, down), (high, up))):
-            ends = (halo[f], own[fields + f])
-            edge[i] = update(
-                halo[fields + f], *(ends if i == 0 else ends[::-1]), lambda n: (we[0, n, i], we[1, n, i]), s
-            )
+            ends = (halo[far], own[near])
+            edge[i] = update(halo[near], *(ends if i == 0 else ends[::-1]), lambda n: (we[0, n, i], we[1, n, i]), s)
         for b in range(boxes):
             load = lambda n: (wm[0, n, b], wm[1, n, b])
             one = pl.ds(b, 1)
             q = state[b, f]
-            q = update(q, *joined(q, low[fields + f, one, :], high[fields + f, one, :]), load, s)
+            q = update(q, *joined(q, low[near, one, :], high[near, one, :]), load, s)
             q = update(q, *joined(q, edge[0, one, :], edge[1, one, :]), load, s)
             res[f, b] = q
-            stay[f, b] = jnp.where(owner[bx * boxes + b] == bx, q, 0.0)
-
-    def to_sibling(t):
+            out[b, k, t] = jnp.where(owner[bx * boxes + b] == bx, q, 0.0)
+
+    def to_sibling(src, dst, t):
         return pltpu.make_async_remote_copy(
-            src_ref=res.at[(1 - core) * half + t],
-            dst_ref=sib.at[t],
-            send_sem=sib_sem.at[0, t],
-            recv_sem=sib_sem.at[1, t],
-            device_id=sibling,
-            device_id_type=MESH,
+            src_ref=src, dst_ref=dst, send_sem=sib_sent.at[0], recv_sem=sib_sem.at[t], device_id=sibling, device_id_type=MESH
         )
 
-    def back(t):
+    def share(t):
+        return to_sibling(res.at[(1 - core) * half + t], sib.at[t], t)
+
+    def back(src, dst):
         return pltpu.make_async_remote_copy(
-            src_ref=fin.at[t],
-            dst_ref=far_out.at[t],
-            send_sem=fin_sem.at[0, t],
-            recv_sem=fin_sem.at[1, t],
-            device_id=sibling,
-            device_id_type=MESH,
+            src_ref=src, dst_ref=dst, send_sem=fin_sem.at[0], recv_sem=fin_sem.at[1], device_id=sibling, device_id_type=MESH
         )
+
+    def kept(k, t):
+        return pltpu.make_async_copy(res.at[k * half + t], res_hbm.at[:, k * half + t], keep_sem.at[k, t])
 
     outgoing, incoming = (sa, sb, sc, sd), (ra, rb, rc, rd)
     start = [2 * sum(CAPS[:i]) for i in range(4)]
@@ -287,23 +281,39 @@
         return pltpu.make_async_remote_copy(
             src_ref=outgoing[stage].at[t, way],
             dst_ref=incoming[stage].at[t, way],
-            send_sem=send.at[stage, way, t],
+            send_sem=send.at[stage],
             recv_sem=recv.at[stage, way, t],
             device_id=around[(stage // 2) * 2 + way],
             device_id_type=MESH,
         )
 
     def compute(t):
+        for way in (0, 1):
+            ends_of(way, 4 * t, 4, t).wait_recv()
+
         @pl.loop(0, 2)
-        def _(i):
-            advance(i * half + t)
-
-        to_sibling(t).start()
+        def _(k):
+            advance(t, k)
+
+        share(t).start()
+        kept(0, t).start()
+        kept(1, t).start()
+
+    def pick(t, first, places, store):
+        for k in range(0, places, 6):
+            group = range(k, min(k + 6, places))
+            values = [pool[t, table[0, first + j]] for j in group]
+            for j, value in zip(group, values):
+                store(j, value)
 
     def gather(stage, t):
+        slots = CAPS[stage]
         for way in (0, 1):
-            for k in range(CAPS[stage]):
-                outgoing[stage][t, way, k] = pool[t, table[0, start[stage] + way * CAPS[stage] + k]]
+
+            def store(k, value, way=way):
+                outgoing[stage][t, way, k] = value
+
+            pick(t, start[stage] + way * slots, slots, store)
             hop(stage, way, t).start()
 
     def take(stage, t):
@@ -312,9 +322,10 @@
             pool[t, pl.ds(16 + start[stage] + way * CAPS[stage], CAPS[stage])] = incoming[stage][t, way]
 
     def first(t):
-        to_sibling(t).wait_recv()
+        share(t).wait_recv()
         pool[t, pl.ds(core * boxes, boxes)] = res[core * half + t]
         pool[t, pl.ds((1 - core) * boxes, boxes)] = sib[t]
+        pool[t, NONE] = jnp.zeros((SIDE, LANES), jnp.float32)
         gather(0, t)
 
     def middle(stage):
@@ -326,18 +337,22 @@
 
     def last(t):
         take(3, t)
-        for dst, whose in ((fin, 1 - core), (near_out, core)):
-
-            @pl.loop(0, homes)
-            def _(h, dst=dst, whose=whose):
-                place = table[0, FINAL + whose * 32 + h]
-                dst[t, h] = jnp.where(place >= 0, pool[t, jnp.maximum(place, 0)], 0.0)
-
-            if dst is fin:
-                back(t).start()
+
+        def store_far(h, value):
+            fin[t, h] = value
+
+        def store_near(h, value):
+            out[boxes + h, core, t] = value
+
+        pick(t, FINAL + (1 - core) * 32, homes, store_far)
+        back(fin.at[t], out.at[pl.ds(boxes, homes), core, t]).start()
+        pick(t, FINAL + core * 32, homes, store_near)
 
     steps = (first, middle(1), middle(2), middle(3), last)
     compute(0)
+    compute(1)
+    to_scalars.wait()
+    lost[0] = table[0, TABLE - 1]
 
     @pl.loop(0, half + len(steps) - 1)
     def _(t):
@@ -347,20 +362,38 @@
             def _(run=run, lag=lag):
                 run(t - lag)
 
-        @pl.when(t + 1 < half)
+        @pl.when(t + 2 < half)
         def _():
-            compute(t + 1)
+            compute(t + 2)
+
+    for way, (src, other) in enumerate(((up, after), (down, before))):
+        pltpu.make_async_remote_copy(
+            src_ref=src,
+            dst_ref=src,
+            send_sem=halo_sent.at[way],
+            recv_sem=halo_sem.at[way, 0],
+            device_id=other,
+            device_id_type=MESH,
+        ).wait_send()
+    to_sibling(sib, sib, 0).wait_send()
+    back(fin, fin).wait()
+    for stage in range(4):
+        pltpu.make_async_remote_copy(
+            src_ref=outgoing[stage],
+            dst_ref=incoming[stage],
+            send_sem=send.at[stage],
+            recv_sem=recv.at[stage, 0, 0],
+            device_id=sibling,
+            device_id_type=MESH,
+        ).wait_send()
 
     @pl.loop(0, half)
     def _(t):
-        to_sibling(t).wait_send()
-        back(t).wait()
-        for stage in range(4):
-            for way in (0, 1):
-                hop(stage, way, t).wait_send()
-
-
-def regrid(table, new_owner, scale, state, kappa, flow):
+        for k in (0, 1):
+            kept(k, t).wait()
+
+
+def regrid(new_owner, scale, state, kappa, flow):
     boxes, fields = state.shape[:2]
     homes = new_owner.shape[0] // boxes
     half = fields // 2
@@ -372,11 +405,15 @@
     dma = pltpu.SemaphoreType.DMA
     return pl.pallas_call(
         functools.partial(regrid_kernel, fields, boxes, homes),
-        out_shape=[jax.ShapeDtypeStruct((fields, boxes) + box, f32)] * 2
-        + [jax.ShapeDtypeStruct((half, homes) + box, f32)] * 2,
-        in_specs=[smem, smem, smem, hbm, hbm, hbm],
-        out_specs=[vmem] * 4,
+        out_shape=[
+            pltpu.VMEM((boxes + homes, 2, half) + box, f32),
+            pltpu.HBM((boxes, fields) + box, f32),
+            jax.ShapeDtypeStruct((1,), I32),
+        ],
+        in_specs=[vmem, smem, smem, hbm, hbm, hbm],
+        out_specs=[vmem, hbm, smem],
         scratch_shapes=[
+            pltpu.VMEM((fields, boxes) + box, f32),
             pltpu.VMEM((boxes, fields) + box, f32),
             pltpu.VMEM((boxes,) + box, f32),
             pltpu.VMEM((boxes, 3) + box, f32),
@@ -388,59 +425,61 @@
             pltpu.VMEM((2, 6, 2, boxes, LANES), f32),
             pltpu.VMEM((2, boxes, LANES), f32),
             pltpu.VMEM((half, boxes) + box, f32),
-            pltpu.VMEM((half, 16 + 2 * sum(CAPS)) + box, f32),
+            pltpu.VMEM((half, NONE + 1) + box, f32),
             pltpu.VMEM((half, homes) + box, f32),
             *slots,
             *slots,
-            dma((3,)),
-            dma((2, 2)),
+            pltpu.VMEM((1, TABLE), I32),
+            pltpu.SMEM((1, TABLE), I32),
+            dma((4,)),
+            dma((2, half + 1)),
+            dma((2,)),
+            dma((half,)),
+            dma((1,)),
+            dma((2,)),
             dma((2, half)),
-            dma((2, half)),
-            dma((4, 2, half)),
+            dma((4,)),
             dma((4, 2, half)),
         ],
-        compiler_params=pltpu.CompilerParams(collective_id=0, has_side_effects=True, vmem_limit_bytes=48 << 20),
+        compiler_params=pltpu.CompilerParams(collective_id=0, has_side_effects=True, vmem_limit_bytes=38 << 20),
         name="regrid",
-    )(table, new_owner, scale, state, kappa, flow)
-
-
-def place_kernel(stay, near, far, out):
-    core = lax.axis_index("bx") % 2
-    boxes = stay.shape[2]
-    for b in range(boxes):
-        for group in (0, 1):
-            out[b, group, 0] = stay[group, 0, b]
-    out[boxes:, core, 0] = near[0]
-    out[boxes:, 1 - core, 0] = far[0]
-
-
-def placed(stay, near, far):
-    fields, boxes = stay.shape[:2]
-    half, homes = near.shape[:2]
-    box = stay.shape[2:]
-    arrived = pl.BlockSpec((1, homes) + box, lambda t: (t, 0, 0, 0))
-    out = pl.pallas_call(
+    )(new_owner.reshape(1, -1), new_owner, scale, state, kappa, flow)
+
+
+def place_kernel(held, out, sem):
+    parts = sem.shape[0]
+    rows = held.shape[0] // parts
+    copies = [
+        pltpu.make_async_copy(held.at[pl.ds(i * rows, rows)], out.at[pl.ds(i * rows, rows)], sem.at[i])
+        for i in range(parts)
+    ]
+    for copy in copies:
+        copy.start()
+    for copy in copies:
+        copy.wait()
+
+
+def placed(held):
+    return pl.pallas_call(
         place_kernel,
-        grid=(half,),
-        out_shape=jax.ShapeDtypeStruct((boxes + homes, 2, half) + box, stay.dtype),
-        in_specs=[pl.BlockSpec((2, 1, boxes) + box, lambda t: (0, t, 0, 0, 0)), arrived, arrived],
-        out_specs=pl.BlockSpec((boxes + homes, 2, 1) + box, lambda t: (0, 0, t, 0, 0)),
-        compiler_params=pltpu.CompilerParams(vmem_limit_bytes=16 << 20),
+        out_shape=pltpu.HBM(held.shape, held.dtype),
+        in_specs=[pl.BlockSpec(memory_space=pltpu.VMEM)],
+        out_specs=pl.BlockSpec(memory_space=pltpu.HBM),
+        scratch_shapes=[pltpu.SemaphoreType.DMA((8,))],
+        compiler_params=pltpu.CompilerParams(vmem_limit_bytes=12 << 20),
         name="placed",
-    )(stay.reshape((2, half, boxes) + box), near, far)
-    return out.reshape((boxes + homes, fields) + box)
+    )(held)
 
 
 def dense(result, new_owner):
     owners, here = lax.axis_size("bx"), lax.axis_index("bx")
-    holding = result.shape[1]
+    holding = result.shape[0]
     local_owner = lax.dynamic_slice_in_dim(new_owner, here * holding, holding)
     moving = local_owner != here
     targets = jnp.arange(owners, dtype=I32)
     picked = (local_owner[None, :] == targets[:, None]) & moving[None, :]
     source = jnp.sum(jnp.where(picked, jnp.arange(holding, dtype=I32)[None, :], 0), axis=1)
     present = jnp.any(picked, axis=1).reshape(owners, 1, 1, 1)
-    result = jnp.swapaxes(result, 0, 1)
     chosen = lax.map(lambda i: lax.dynamic_index_in_dim(result, i, 0, keepdims=False), source)
     arrived = lax.all_to_all(jnp.where(present, chosen, 0.0), "bx", split_axis=0, concat_axis=0, tiled=True)
     staying = jnp.logical_not(moving).reshape(holding, 1, 1, 1)
@@ -448,18 +487,10 @@
 
 
 def on_device(state, diffusivity, velocity, species_scale, new_owner):
-    table = make_plan(new_owner)
-    res, stay, near, far = regrid(table, new_owner, species_scale, state[0], diffusivity[0], velocity[0])
-    result = lax.cond(
-        table[0, TABLE - 1] == 0,
-        lambda res, stay, near, far: placed(stay, near, far),
-        lambda res, stay, near, far: dense(res, new_owner),
-        res,
-        stay,
-        near,
-        far,
-    )
-    return result[None]
+    inputs = (pltpu.with_memory_space_constraint(x[0], pltpu.HBM) for x in (state, diffusivity, velocity))
+    held, res, lost = regrid(new_owner, species_scale, *inputs)
+    out = placed(held).reshape((held.shape[0],) + state.shape[2:])
+    return lax.fori_loop(0, lost[0], lambda _, out: dense(res, new_owner), out)[None]
 
 
 def solution(mesh):

time: 97.8 us -> 74.4 us (0.76)
  Pallas kernels: 87.7 us -> 72 us
  local copies, waits for them, and re-layouts: 8.96 us -> 0.66 us
    pallas_call x1, Pallas kernels: 77 us -> 68.4 us  [regrid(): pl.pallas_call(functools.partial(regrid_kernel, fields, boxes, homes), ou...]
    unnamed x12 -> x4, local copies, waits for them, and re-layouts: 8.38 us -> 0.66 us
    pallas_call x2 -> x1, Pallas kernels: 10.7 us -> 3.62 us  [placed(): pl.pallas_call(place_kernel, out_shape=pltpu.HBM(held.shape, held.dtype),...]
where the time goes in v3:
time: 74.4 us; the launch traced here: 74.2 us
  Pallas kernels  72 us (97%)
  other arithmetic  0.93 us (1%)
    pallas_call x1, Pallas kernels, regrid(): pl.pallas_call(functools.partial(regrid_kernel, fields, boxes, homes), ou...  68.4 us
    pallas_call x1, Pallas kernels, placed(): pl.pallas_call(place_kernel, out_shape=pltpu.HBM(held.shape, held.dtype),...  3.62 us

profile of v3, /device:TPU:1, one launch (start us, length us, event | category | flops | bytes accessed | tf_op | source)
XLA Modules:
  0.0 74.2 jit_solution(11424039104648056092)
XLA Ops:
  0.0 0.8 %broadcast_compare_fusion = (pred[8]{0:T(512)(128)(4,1)S(1)}, s32[8]{0:T(128)S(1)}) fusion(s32[]{:T(128)S(6)} %axis_index.22, s32[256]{0:T(256)} %owner.1, s32[]{:T(128)S(6)} %select_n.27), kind=kLoop, calls=%fused_computation.9 | loop fusion | flops 8 | bytes 80 | tf_op jit(solution)/shard_map/while/body/ne | solution.py:478
  0.8 0.1 select_reduce_fusion
  0.8 0.1 fusion.1
  0.9 0.0 copy-start
  0.9 0.7 copy-done
  1.6 68.4 %regrid.1 = (f32[40,2,7,16,256]{4,3,2,1,0:T(8,128)S(1)}, f32[8,14,16,256]{3,2,1,0:T(8,128)}, s32[1]{0:T(128)}) custom-call(s32[1,256]{1,0:T(1,128)} %bitcast.14, s32[256]{0:T(256)} %owner.1, f32[14]{0:T(128)S(1)} %copy-done, f32[8,14,16,256]{3,2,1,0:T(8,128)} %bitcast.11, f32[8,16,256]{2,1,0:T(8,128)} %bitcast.13, f32[8,3,16,256]{3,2,1,0:T(8,128)} %bitcast.12), custom_call_target="tpu_custom_call" | custom-call | tf_op jit(solution)/shard_map/regrid/pallas_call | solution.py:406
  70.0 0.0 copy-start.1
  70.0 3.6 %placed.1 = f32[40,2,7,16,256]{4,3,2,1,0:T(8,128)} custom-call(f32[40,2,7,16,256]{4,3,2,1,0:T(8,128)S(1)} %get-tuple-element.85.held), custom_call_target="tpu_custom_call" | custom-call | tf_op jit(solution)/shard_map/placed/pallas_call | solution.py:463
  73.6 0.0 copy-done.1
  73.6 0.6 while.28
Async XLA Ops:
  0.9 0.7 copy-start
  70.0 3.6 %copy-start.1 = (s32[256]{0:T(256)S(1)}, s32[256]{0:T(256)}, u32[]{:S(2)}) copy-start(s32[256]{0:T(256)} %owner.1) | copy-start | bytes 3076

commit v4 on v3

--- a/solution.py
+++ b/solution.py
@@ -56,8 +56,10 @@
 
 
 I32 = jnp.int32
-CAPS = (7, 6, 11, 8)
+CAPS = (6, 5, 10, 7)
+LAGS = (0, 2, 4, 6, 8)
 RING = 4
+NODES = RING * RING
 TABLE = 256
 FINAL = 128
 NONE = 16 + 2 * sum(CAPS)
@@ -73,19 +75,42 @@
     return jnp.sum(jnp.where(eye, row, 0), axis=1, keepdims=True)
 
 
-def hops(at, d, node_up, node_down, first, second):
+def node_values(values, at):
+    across = lax.broadcasted_iota(I32, (NODES, 128), 0) == lax.broadcasted_iota(I32, (NODES, 128), 1)
+    values = jnp.sum(jnp.where(across, values, 0), axis=1, keepdims=True)
+    there = lax.broadcasted_iota(I32, (NODES, at.shape[1]), 0) == at
+    return jnp.sum(jnp.where(there, values, 0), axis=0, keepdims=True)
+
+
+def balanced(n1, n2, n3, most):
+    up = lambda x: pltpu.roll(x, 128 - RING, 1)
+    down = lambda x: pltpu.roll(x, RING, 1)
+    place = lax.broadcasted_iota(I32, n1.shape, 1) // RING % 2
+    within = lambda x: jnp.minimum(jnp.maximum(x, jnp.maximum(n2 - most, 0)), jnp.minimum(n2, most))
+    half = within((n2 + n3 - n1 + 1) >> 1)
+    for turn in (0, 1):
+        rest = n2 - half
+        with_up = jnp.maximum(n1 + down(half), up(n1) + up(half))
+        with_down = jnp.maximum(n3 + up(rest), down(n3) + down(rest))
+        half = jnp.where(place == turn, within((with_down + n2 - with_up + 1) >> 1), half)
+    return half
+
+
+def hops(at, d, first, second):
     n = at.shape[1]
     earlier = lax.broadcasted_iota(I32, (n, n), 0) < lax.broadcasted_iota(I32, (n, n), 1)
     at_c, d_c = column(at), column(d)
-    here = at_c == at
+    r = count((at_c == at) & (d_c == d) & earlier)
+    here = at_c == lax.broadcasted_iota(I32, (n, 128), 1) % NODES
     n1, n2, n3 = (count(here & (d_c == k)) for k in (1, 2, 3))
-    r = count(here & (d_c == d) & earlier)
-    half = jnp.clip((n2 + n3 - n1 + 1) >> 1, 0, n2)
+    half = balanced(n1, n2, n3, min(first, second))
+    node_up, node_down = (at + RING) % NODES, (at + NODES - RING) % NODES
+    ups, downs = node_values(half, at), node_values(n2 - half, at)
     two = d == 2
-    up = jnp.where(two, jnp.where(r < half, 1, 0), jnp.where(d == 1, 1, 0))
-    rank = jnp.where(two, jnp.where(r < half, r, r - half), jnp.where(d == 1, half + r, n2 - half + r))
+    up = jnp.where(two, jnp.where(r < ups, 1, 0), jnp.where(d == 1, 1, 0))
+    rank = jnp.where(two, jnp.where(r < ups, r, r - ups), jnp.where(d == 1, ups + r, downs + r))
     mid = jnp.where(up == 1, node_up, node_down)
-    local = count((at_c == mid) & (column(up) == up) & (d_c > 0))
+    local = jnp.where(up == 1, node_values(n1 + half, node_up), node_values(n3 + n2 - half, node_down))
     late = rank >= first
     slot = jnp.where(two, jnp.maximum(local - first, 0) + rank, rank - first)
     lost = (two & (late | (slot >= second))) | ((d > 0) & jnp.logical_not(two) & (slot >= second))
@@ -105,7 +130,8 @@
     node = lambda p, q: p * RING + q
     p0, q0 = pq(home // 2)
     p1, q1 = pq(jnp.where(moving, owner, home) // 2)
-    me = node(y, z) if net == 0 else node(z, y)
+    my_p, my_q = (y, z) if net == 0 else (z, y)
+    me, me2 = node(my_p, my_q), node(my_q, my_p)
     turn = lambda p, k: (p + k) % RING
     base_a = 16
     base_b = base_a + 2 * ka
@@ -113,26 +139,22 @@
     base_d = base_c + 2 * kc
     own = b % 16
     d1 = turn(p1 - p0, RING)
-    up1, rank1, late1, slot1, mid1, lost1 = hops(
-        node(p0, q0), d1, node(turn(p0, 1), q0), node(turn(p0, 3), q0), ka, kb
-    )
+    up1, rank1, late1, slot1, mid1, lost1 = hops(node(p0, q0), d1, ka, kb)
     in_a = base_a + (1 - up1) * ka + rank1
     at1 = jnp.where(d1 == 0, own, jnp.where((d1 == 2) | late1, base_b + (1 - up1) * kb + slot1, in_a))
     d2 = turn(q1 - q0, RING)
-    up2, rank2, late2, slot2, mid2, lost2 = hops(
-        node(p1, q0), d2, node(p1, turn(q0, 1)), node(p1, turn(q0, 3)), kc, kd
-    )
+    up2, rank2, late2, slot2, mid2, lost2 = hops(node(q0, p1), d2, kc, kd)
     in_c = base_c + (1 - up2) * kc + rank2
     at2 = jnp.where(d2 == 0, at1, jnp.where((d2 == 2) | late2, base_d + (1 - up2) * kd + slot2, in_c))
-    nodes = (node(p0, q0), node(p1, q0), node(p1, q1))
+    nodes = (node(p0, q0), node(q0, p1), node(q1, p1))
     entries = (
         ((nodes[0] == me) & (d1 > 0) & jnp.logical_not(late1), (1 - up1) * ka + rank1, own),
         ((nodes[0] == me) & (d1 > 0) & (d1 != 2) & late1, 2 * ka + (1 - up1) * kb + slot1, own),
         ((mid1 == me) & (d1 == 2), 2 * ka + (1 - up1) * kb + slot1, in_a),
-        ((nodes[1] == me) & (d2 > 0) & jnp.logical_not(late2), 2 * (ka + kb) + (1 - up2) * kc + rank2, at1),
-        ((nodes[1] == me) & (d2 > 0) & (d2 != 2) & late2, 2 * (ka + kb + kc) + (1 - up2) * kd + slot2, at1),
-        ((mid2 == me) & (d2 == 2), 2 * (ka + kb + kc) + (1 - up2) * kd + slot2, in_c),
-        ((nodes[2] == me) & moving, FINAL + (owner % 2) * 32 + home, at2 - NONE),
+        ((nodes[1] == me2) & (d2 > 0) & jnp.logical_not(late2), 2 * (ka + kb) + (1 - up2) * kc + rank2, at1),
+        ((nodes[1] == me2) & (d2 > 0) & (d2 != 2) & late2, 2 * (ka + kb + kc) + (1 - up2) * kd + slot2, at1),
+        ((mid2 == me2) & (d2 == 2), 2 * (ka + kb + kc) + (1 - up2) * kd + slot2, in_c),
+        ((nodes[2] == me2) & moving, FINAL + (owner % 2) * 32 + home, at2 - NONE),
     )
     lane = lax.broadcasted_iota(I32, (n, TABLE), 1)
     table = jnp.where(lax.broadcasted_iota(I32, (1, TABLE), 1) >= FINAL, NONE, 0)
@@ -354,9 +376,9 @@
     to_scalars.wait()
     lost[0] = table[0, TABLE - 1]
 
-    @pl.loop(0, half + len(steps) - 1)
+    @pl.loop(0, half + LAGS[-1])
     def _(t):
-        for lag, run in enumerate(steps):
+        for lag, run in zip(LAGS, steps):
 
             @pl.when((t >= lag) & (t < half + lag))
             def _(run=run, lag=lag):

time: 74.4 us -> 64.4 us (0.87)
  Pallas kernels: 72 us -> 62 us
    pallas_call x1, Pallas kernels: 68.4 us -> 58.4 us  [regrid(): pl.pallas_call(functools.partial(regrid_kernel, fields, boxes, homes), ou...]
where the time goes in v4:
time: 64.4 us; the launch traced here: 64.2 us
  Pallas kernels  62 us (96%)
  other arithmetic  0.93 us (1%)
  local copies, waits for them, and re-layouts  0.66 us (1%)
    pallas_call x1, Pallas kernels, regrid(): pl.pallas_call(functools.partial(regrid_kernel, fields, boxes, homes), ou...  58.4 us
    pallas_call x1, Pallas kernels, placed(): pl.pallas_call(place_kernel, out_shape=pltpu.HBM(held.shape, held.dtype),...  3.62 us

profile of v4, /device:TPU:1, one launch (start us, length us, event | category | flops | bytes accessed | tf_op | source)
XLA Modules:
  0.0 64.2 jit_solution(6806852116788213040)
XLA Ops:
  0.0 0.8 %broadcast_compare_fusion = (pred[8]{0:T(512)(128)(4,1)S(1)}, s32[8]{0:T(128)S(1)}) fusion(s32[]{:T(128)S(6)} %axis_index.22, s32[256]{0:T(256)} %owner.1, s32[]{:T(128)S(6)} %select_n.27), kind=kLoop, calls=%fused_computation.9 | loop fusion | flops 8 | bytes 80 | tf_op jit(solution)/shard_map/while/body/ne | solution.py:500
  0.8 0.1 select_reduce_fusion
  0.8 0.1 fusion.1
  0.9 0.0 copy-start
  0.9 0.7 %copy-done = f32[14]{0:T(128)S(1)} copy-done((f32[14]{0:T(128)S(1)}, f32[14]{0:T(128)}, u32[]{:S(2)}) %copy-start) | copy-done | bytes 80
  1.6 58.4 %regrid.1 = (f32[40,2,7,16,256]{4,3,2,1,0:T(8,128)S(1)}, f32[8,14,16,256]{3,2,1,0:T(8,128)}, s32[1]{0:T(128)}) custom-call(s32[1,256]{1,0:T(1,128)} %bitcast.14, s32[256]{0:T(256)} %owner.1, f32[14]{0:T(128)S(1)} %copy-done, f32[8,14,16,256]{3,2,1,0:T(8,128)} %bitcast.11, f32[8,16,256]{2,1,0:T(8,128)} %bitcast.13, f32[8,3,16,256]{3,2,1,0:T(8,128)} %bitcast.12), custom_call_target="tpu_custom_call" | custom-call | tf_op jit(solution)/shard_map/regrid/pallas_call | solution.py:428
  60.0 0.0 copy-start.1
  60.0 3.6 %placed.1 = f32[40,2,7,16,256]{4,3,2,1,0:T(8,128)} custom-call(f32[40,2,7,16,256]{4,3,2,1,0:T(8,128)S(1)} %get-tuple-element.85.held), custom_call_target="tpu_custom_call" | custom-call | tf_op jit(solution)/shard_map/placed/pallas_call | solution.py:485
  63.6 0.0 copy-done.1
  63.6 0.6 while.28
Async XLA Ops:
  0.9 0.7 %copy-start = (f32[14]{0:T(128)S(1)}, f32[14]{0:T(128)}, u32[]{:S(2)}) copy-start(f32[14]{0:T(128)} %scale.1) | copy-start | bytes 172
  60.0 3.6 %copy-start.1 = (s32[256]{0:T(256)S(1)}, s32[256]{0:T(256)}, u32[]{:S(2)}) copy-start(s32[256]{0:T(256)} %owner.1) | copy-start | bytes 3076

commit v5 on v4

--- a/solution.py
+++ b/solution.py
@@ -28,23 +28,25 @@
     return q + spread
 
 
-def weights(k, k_behind, k_ahead, u, v, w, store):
+def weight(k, other, speed, up, inside=None):
+    a = (0.5 * time_step) * (k + other)
+    b = (-time_step) * jnp.minimum(speed, 0.0) if up else time_step * jnp.maximum(speed, 0.0)
+    if inside is not None:
+        a, b = jnp.where(inside, a, 0.0), jnp.where(inside, b, 0.0)
+    return a, b
+
+
+def weights_x(k, k_behind, k_ahead, u, store):
+    for n, other in enumerate((k_behind, k_ahead)):
+        store(n, *weight(k, other, u, n == 1))
+
+
+def weights_yz(k, v, w, store):
     lane = lax.broadcasted_iota(jnp.int32, k.shape, k.ndim - 1)
     y, z = lane // SIDE, lane % SIDE
-    sides = (
-        (k_behind, u, False, None),
-        (k_ahead, u, True, None),
-        (moved(k, -SIDE), v, False, y > 0),
-        (moved(k, SIDE), v, True, y < SIDE - 1),
-        (moved(k, -1), w, False, z > 0),
-        (moved(k, 1), w, True, z < SIDE - 1),
-    )
-    for n, (other, speed, up, inside) in enumerate(sides):
-        a = (0.5 * time_step) * (k + other)
-        b = (-time_step) * jnp.minimum(speed, 0.0) if up else time_step * jnp.maximum(speed, 0.0)
-        if inside is not None:
-            a, b = jnp.where(inside, a, 0.0), jnp.where(inside, b, 0.0)
-        store(n, a, b)
+    sides = ((-SIDE, v, y > 0), (SIDE, v, y < SIDE - 1), (-1, w, z > 0), (1, w, z < SIDE - 1))
+    for n, (shift, speed, inside) in enumerate(sides):
+        store(2 + n, *weight(k, moved(k, shift), speed, shift > 0, inside))
 
 
 def joined(q, first, last):
@@ -58,6 +60,8 @@
 I32 = jnp.int32
 CAPS = (6, 5, 10, 7)
 LAGS = (0, 2, 4, 6, 8)
+PIECES = 1
+ROWS = SIDE // PIECES
 RING = 4
 NODES = RING * RING
 TABLE = 256
@@ -118,7 +122,6 @@
 
 
 def plan(owner, z, y, net):
-    n = owner.shape[1]
     ka, kb, kc, kd = CAPS
     b = lax.broadcasted_iota(I32, owner.shape, 1)
     home = b // 8
@@ -156,26 +159,30 @@
         ((mid2 == me2) & (d2 == 2), 2 * (ka + kb + kc) + (1 - up2) * kd + slot2, in_c),
         ((nodes[2] == me2) & moving, FINAL + (owner % 2) * 32 + home, at2 - NONE),
     )
-    lane = lax.broadcasted_iota(I32, (n, TABLE), 1)
-    table = jnp.where(lax.broadcasted_iota(I32, (1, TABLE), 1) >= FINAL, NONE, 0)
-    for mask, slot, place in entries:
-        slot, place = column(jnp.where(mask, slot, -1)), column(place)
-        table = table + jnp.sum(jnp.where(lane == slot, place, 0), axis=0, keepdims=True)
-    return jnp.clip(table, 0, NONE), lost1 + lost2
+    return [(jnp.where(mask, slot, -1), place) for mask, slot, place in entries], lost1 + lost2
 
 
 def both_plans(owner, z, y, core):
+    n = owner.shape[1]
     one, lost_one = plan(owner, z, y, 0)
     two, lost_two = plan(owner, z, y, 1)
-    row = jnp.where(core == 0, one, two)
+    number = lax.broadcasted_iota(I32, (TABLE, n), 0)
+    table = jnp.zeros((TABLE, n), I32)
+    for (slot_one, place_one), (slot_two, place_two) in zip(one, two):
+        slot, place = jnp.where(core == 0, slot_one, slot_two), jnp.where(core == 0, place_one, place_two)
+        table = table + jnp.where(number == slot, place, 0)
+    table = jnp.sum(table, axis=1, keepdims=True)
+    eye = lax.broadcasted_iota(I32, (TABLE, TABLE), 0) == lax.broadcasted_iota(I32, (TABLE, TABLE), 1)
+    row = jnp.sum(jnp.where(eye, table, 0), axis=0, keepdims=True)
     lane = lax.broadcasted_iota(I32, row.shape, 1)
+    row = jnp.clip(row + jnp.where(lane >= FINAL, NONE, 0), 0, NONE)
     return jnp.where(lane == TABLE - 1, jnp.broadcast_to(jnp.minimum(lost_one + lost_two, 1), row.shape), row)
 
 
 def regrid_kernel(
-    fields, boxes, homes, owner_row, owner, scale, state_hbm, kappa_hbm, flow_hbm, out, res_hbm, lost,
+    fields, boxes, homes, owner_row, owner_hbm, scale_hbm, state_hbm, kappa_hbm, flow_hbm, out, res_hbm, lost,
     res, state, kappa, flow, up, down, low, high, wm, we, edge, sib, pool, fin, sa, sb, sc, sd, ra, rb, rc, rd,
-    row, table, in_sem, halo_sem, halo_sent, sib_sem, sib_sent, fin_sem, keep_sem, send, recv,
+    row, table, owner, scale, in_sem, halo_sem, halo_sent, sib_sem, sib_sent, fin_sem, keep_sem, send, recv,
 ):
     xs, bx, n_xs = lax.axis_index("xs"), lax.axis_index("bx"), lax.axis_size("xs")
     chip, core = bx // 2, bx % 2
@@ -197,7 +204,9 @@
         pl.semaphore_signal(barrier, inc=1, device_id=other, device_id_type=MESH)
     loads = [
         pltpu.make_async_copy(src, dst, in_sem.at[i])
-        for i, (src, dst) in enumerate(((state_hbm, state), (kappa_hbm, kappa), (flow_hbm, flow)))
+        for i, (src, dst) in enumerate(
+            ((state_hbm, state), (kappa_hbm, kappa), (flow_hbm, flow), (owner_hbm, owner), (scale_hbm, scale))
+        )
     ]
     for copy in loads:
         copy.start()
@@ -238,17 +247,12 @@
     for copy in coefficients:
         copy.start()
 
-    @pl.loop(0, half)
-    def _(t):
+    def send_ends(t):
         for way in (0, 1):
             ends_of(way, 4 * t, 4, t).start()
 
-    row[...] = both_plans(owner_row[...], z, y, core)
-    to_scalars = pltpu.make_async_copy(row, table, in_sem.at[3])
-    to_scalars.start()
-    for copy in coefficients:
-        copy.wait_recv()
-
+    send_ends(0)
+    send_ends(1)
     def keep(ref, at):
         def store(n, a, b):
             ref[(0, n) + at] = a
@@ -256,13 +260,26 @@
 
         return store
 
-    for i, (far, near, own) in enumerate(((low, low, down), (high, high, up))):
-        ends = (far[far_k], own[near_k])
-        weights(near[near_k], *(ends if i == 0 else ends[::-1]), *(near[near_v + d] for d in range(3)), keep(we, (i,)))
+    row[...] = both_plans(owner_row[...], z, y, core)
+    to_scalars = pltpu.make_async_copy(row, table, in_sem.at[5])
+    to_scalars.start()
+    for b in range(boxes):
+        weights_yz(kappa[b], flow[b, 1], flow[b, 2], keep(wm, (b,)))
+    for copy in coefficients:
+        copy.wait_recv()
+
+    @pl.loop(2, half)
+    def _(t):
+        send_ends(t)
+
+    for i, (halo, own) in enumerate(((low, down), (high, up))):
+        k, ends = halo[near_k], (halo[far_k], own[near_k])
+        weights_x(k, *(ends if i == 0 else ends[::-1]), halo[near_v], keep(we, (i,)))
+        weights_yz(k, halo[near_v + 1], halo[near_v + 2], keep(we, (i,)))
     for b in range(boxes):
         k = kappa[b]
         behind, ahead = joined(k, low[near_k, pl.ds(b, 1), :], high[near_k, pl.ds(b, 1), :])
-        weights(k, behind, ahead, flow[b, 0], flow[b, 1], flow[b, 2], keep(wm, (b,)))
+        weights_x(k, behind, ahead, flow[b, 0], keep(wm, (b,)))
 
     def advance(t, k):
         f = k * half + t
@@ -285,8 +302,12 @@
             src_ref=src, dst_ref=dst, send_sem=sib_sent.at[0], recv_sem=sib_sem.at[t], device_id=sibling, device_id_type=MESH
         )
 
-    def share(t):
-        return to_sibling(res.at[(1 - core) * half + t], sib.at[t], t)
+    def rows_of(part):
+        return part // PIECES, pl.ds(pl.multiple_of(part % PIECES * ROWS, ROWS), ROWS)
+
+    def share(part):
+        t, rows = rows_of(part)
+        return to_sibling(res.at[(1 - core) * half + t, :, rows], sib.at[part], part)
 
     def back(src, dst):
         return pltpu.make_async_remote_copy(
@@ -317,13 +338,14 @@
         def _(k):
             advance(t, k)
 
-        share(t).start()
+        for piece in range(PIECES):
+            share(t * PIECES + piece).start()
         kept(0, t).start()
         kept(1, t).start()
 
     def pick(t, first, places, store):
-        for k in range(0, places, 6):
-            group = range(k, min(k + 6, places))
+        for k in range(0, places, 6 * PIECES):
+            group = range(k, min(k + 6 * PIECES, places))
             values = [pool[t, table[0, first + j]] for j in group]
             for j, value in zip(group, values):
                 store(j, value)
@@ -343,12 +365,13 @@
             hop(stage, way, t).wait_recv()
             pool[t, pl.ds(16 + start[stage] + way * CAPS[stage], CAPS[stage])] = incoming[stage][t, way]
 
-    def first(t):
-        share(t).wait_recv()
-        pool[t, pl.ds(core * boxes, boxes)] = res[core * half + t]
-        pool[t, pl.ds((1 - core) * boxes, boxes)] = sib[t]
-        pool[t, NONE] = jnp.zeros((SIDE, LANES), jnp.float32)
-        gather(0, t)
+    def first(part):
+        share(part).wait_recv()
+        t, rows = rows_of(part)
+        pool[part, pl.ds(core * boxes, boxes)] = res[core * half + t, :, rows]
+        pool[part, pl.ds((1 - core) * boxes, boxes)] = sib[part]
+        pool[part, NONE] = jnp.zeros((ROWS, LANES), jnp.float32)
+        gather(0, part)
 
     def middle(stage):
         def run(t):
@@ -357,18 +380,19 @@
 
         return run
 
-    def last(t):
-        take(3, t)
+    def last(part):
+        take(3, part)
+        t, rows = rows_of(part)
 
         def store_far(h, value):
-            fin[t, h] = value
+            fin[part, h] = value
 
         def store_near(h, value):
-            out[boxes + h, core, t] = value
-
-        pick(t, FINAL + (1 - core) * 32, homes, store_far)
-        back(fin.at[t], out.at[pl.ds(boxes, homes), core, t]).start()
-        pick(t, FINAL + core * 32, homes, store_near)
+            out[boxes + h, core, t, rows] = value
+
+        pick(part, FINAL + (1 - core) * 32, homes, store_far)
+        back(fin.at[part], out.at[pl.ds(boxes, homes), core, t, rows]).start()
+        pick(part, FINAL + core * 32, homes, store_near)
 
     steps = (first, middle(1), middle(2), middle(3), last)
     compute(0)
@@ -376,17 +400,19 @@
     to_scalars.wait()
     lost[0] = table[0, TABLE - 1]
 
-    @pl.loop(0, half + LAGS[-1])
+    parts = half * PIECES
+
+    @pl.loop(0, parts + LAGS[-1])
     def _(t):
         for lag, run in zip(LAGS, steps):
 
-            @pl.when((t >= lag) & (t < half + lag))
+            @pl.when((t >= lag) & (t < parts + lag))
             def _(run=run, lag=lag):
                 run(t - lag)
 
-        @pl.when(t + 2 < half)
+        @pl.when((t % PIECES == 0) & (t // PIECES + 2 < half))
         def _():
-            compute(t + 2)
+            compute(t // PIECES + 2)
 
     for way, (src, other) in enumerate(((up, after), (down, before))):
         pltpu.make_async_remote_copy(
@@ -415,7 +441,7 @@
             kept(k, t).wait()
 
 
-def regrid(new_owner, scale, state, kappa, flow):
+def regrid(owner_row, new_owner, scale, state, kappa, flow):
     boxes, fields = state.shape[:2]
     homes = new_owner.shape[0] // boxes
     half = fields // 2
@@ -423,7 +449,8 @@
     vmem, smem, hbm = (pl.BlockSpec(memory_space=m) for m in (pltpu.VMEM, pltpu.SMEM, pltpu.HBM))
     box = (SIDE, LANES)
     halo = pltpu.VMEM((2 * fields + 5, boxes, LANES), f32)
-    slots = [pltpu.VMEM((half, 2, k) + box, f32) for k in CAPS]
+    parts, piece = half * PIECES, (ROWS, LANES)
+    slots = [pltpu.VMEM((parts, 2, k) + piece, f32) for k in CAPS]
     dma = pltpu.SemaphoreType.DMA
     return pl.pallas_call(
         functools.partial(regrid_kernel, fields, boxes, homes),
@@ -432,7 +459,7 @@
             pltpu.HBM((boxes, fields) + box, f32),
             jax.ShapeDtypeStruct((1,), I32),
         ],
-        in_specs=[vmem, smem, smem, hbm, hbm, hbm],
+        in_specs=[vmem, hbm, hbm, hbm, hbm, hbm],
         out_specs=[vmem, hbm, smem],
         scratch_shapes=[
             pltpu.VMEM((fields, boxes) + box, f32),
@@ -446,26 +473,28 @@
             pltpu.VMEM((2, 6, boxes) + box, f32),
             pltpu.VMEM((2, 6, 2, boxes, LANES), f32),
             pltpu.VMEM((2, boxes, LANES), f32),
-            pltpu.VMEM((half, boxes) + box, f32),
-            pltpu.VMEM((half, NONE + 1) + box, f32),
-            pltpu.VMEM((half, homes) + box, f32),
+            pltpu.VMEM((parts, boxes) + piece, f32),
+            pltpu.VMEM((parts, NONE + 1) + piece, f32),
+            pltpu.VMEM((parts, homes) + piece, f32),
             *slots,
             *slots,
             pltpu.VMEM((1, TABLE), I32),
             pltpu.SMEM((1, TABLE), I32),
-            dma((4,)),
+            pltpu.SMEM(new_owner.shape, I32),
+            pltpu.SMEM(scale.shape, f32),
+            dma((6,)),
             dma((2, half + 1)),
             dma((2,)),
-            dma((half,)),
+            dma((parts,)),
             dma((1,)),
             dma((2,)),
             dma((2, half)),
             dma((4,)),
-            dma((4, 2, half)),
+            dma((4, 2, parts)),
         ],
         compiler_params=pltpu.CompilerParams(collective_id=0, has_side_effects=True, vmem_limit_bytes=38 << 20),
         name="regrid",
-    )(new_owner.reshape(1, -1), new_owner, scale, state, kappa, flow)
+    )(owner_row, new_owner, scale, state, kappa, flow)
 
 
 def place_kernel(held, out, sem):
@@ -502,17 +531,27 @@
     picked = (local_owner[None, :] == targets[:, None]) & moving[None, :]
     source = jnp.sum(jnp.where(picked, jnp.arange(holding, dtype=I32)[None, :], 0), axis=1)
     present = jnp.any(picked, axis=1).reshape(owners, 1, 1, 1)
-    chosen = lax.map(lambda i: lax.dynamic_index_in_dim(result, i, 0, keepdims=False), source)
+    chosen = result[:1]
+    for b in range(1, holding):
+        chosen = jnp.where((source == b).reshape(owners, 1, 1, 1), result[b], chosen)
     arrived = lax.all_to_all(jnp.where(present, chosen, 0.0), "bx", split_axis=0, concat_axis=0, tiled=True)
     staying = jnp.logical_not(moving).reshape(holding, 1, 1, 1)
     return jnp.concatenate([jnp.where(staying, result, 0.0), arrived], axis=0)
 
 
 def on_device(state, diffusivity, velocity, species_scale, new_owner):
-    inputs = (pltpu.with_memory_space_constraint(x[0], pltpu.HBM) for x in (state, diffusivity, velocity))
-    held, res, lost = regrid(new_owner, species_scale, *inputs)
+    inputs = (
+        pltpu.with_memory_space_constraint(x, pltpu.HBM)
+        for x in (new_owner, species_scale, state[0], diffusivity[0], velocity[0])
+    )
+    held, res, lost = regrid(new_owner.reshape(1, -1), *inputs)
     out = placed(held).reshape((held.shape[0],) + state.shape[2:])
-    return lax.fori_loop(0, lost[0], lambda _, out: dense(res, new_owner), out)[None]
+
+    def again(i, out):
+        _, owner = lax.optimization_barrier((i, new_owner))
+        return dense(res, owner)
+
+    return lax.fori_loop(0, lost[0], again, out)[None]
 
 
 def solution(mesh):

time: 64.4 us -> 61.7 us (0.958)
  Pallas kernels: 62 us -> 61 us
  other arithmetic: 0.93 us -> 0 us
  local copies, waits for them, and re-layouts: 0.66 us -> 0.01 us
    pallas_call x1, Pallas kernels: 58.4 us -> 57.4 us  [regrid(): pl.pallas_call(functools.partial(regrid_kernel, fields, boxes, homes), ou...]
    ne x1 -> x0, other arithmetic: 0.75 us -> none  [dense(): moving = local_owner != here]
    unnamed x4 -> x2, local copies, waits for them, and re-layouts: 0.66 us -> 0.01 us
where the time goes in v5:
time: 61.7 us; the launch traced here: 61.6 us
  Pallas kernels  61 us (99%)
    pallas_call x1, Pallas kernels, regrid(): pl.pallas_call(functools.partial(regrid_kernel, fields, boxes, homes), ou...  57.4 us
    pallas_call x1, Pallas kernels, placed(): pl.pallas_call(place_kernel, out_shape=pltpu.HBM(held.shape, held.dtype),...  3.62 us

profile of v5, /device:TPU:1, one launch (start us, length us, event | category | flops | bytes accessed | tf_op | source)
XLA Modules:
  0.0 61.6 jit_solution(9635887001332502694)
XLA Ops:
  0.0 57.4 %regrid.1 = (f32[40,2,7,16,256]{4,3,2,1,0:T(8,128)S(1)}, f32[8,14,16,256]{3,2,1,0:T(8,128)}, s32[1]{0:T(128)}) custom-call(s32[1,256]{1,0:T(1,128)} %bitcast.29, s32[256]{0:T(256)} %owner_hbm.1, f32[14]{0:T(128)} %scale_hbm.1, f32[8,14,16,256]{3,2,1,0:T(8,128)} %bitcast.26, f32[8,16,256]{2,1,0:T(8,128)} %bitcast.28, f32[8,3,16,256]{3,2,1,0:T(8,128)} %bitcast.27), custom_call_target="tpu_custom_call" | custom-call | tf_op jit(solution)/shard_map/regrid/pallas_call | solution.py:455
  57.4 0.0 copy-start
  57.4 3.6 %placed.1 = f32[40,2,7,16,256]{4,3,2,1,0:T(8,128)} custom-call(f32[40,2,7,16,256]{4,3,2,1,0:T(8,128)S(1)} %get-tuple-element.36.held), custom_call_target="tpu_custom_call" | custom-call | tf_op jit(solution)/shard_map/placed/pallas_call | solution.py:514
  61.0 0.0 copy-done
  61.0 0.6 while.10
Async XLA Ops:
  57.4 3.6 %copy-start = (s32[256]{0:T(256)S(1)}, s32[256]{0:T(256)}, u32[]{:S(2)}) copy-start(s32[256]{0:T(256)} %owner_hbm.1) | copy-start | bytes 3076

commit v6 on v5

--- a/solution.py
+++ b/solution.py
@@ -410,9 +410,11 @@
             def _(run=run, lag=lag):
                 run(t - lag)
 
-        @pl.when((t % PIECES == 0) & (t // PIECES + 2 < half))
-        def _():
-            compute(t // PIECES + 2)
+            if lag == 0:
+
+                @pl.when((t % PIECES == 0) & (t // PIECES + 2 < half))
+                def _():
+                    compute(t // PIECES + 2)
 
     for way, (src, other) in enumerate(((up, after), (down, before))):
         pltpu.make_async_remote_copy(

time: 61.7 us -> 61.2 us (level)
  no operation moved by 1% of the time
where the time goes in v6:
time: 61.2 us; the launch traced here: 61 us
  Pallas kernels  60.4 us (99%)
    pallas_call x1, Pallas kernels, regrid(): pl.pallas_call(functools.partial(regrid_kernel, fields, boxes, homes), ou...  56.8 us
    pallas_call x1, Pallas kernels, placed(): pl.pallas_call(place_kernel, out_shape=pltpu.HBM(held.shape, held.dtype),...  3.62 us

profile of v6, /device:TPU:1, one launch (start us, length us, event | category | flops | bytes accessed | tf_op | source)
XLA Modules:
  0.0 61.0 jit_solution(16982845431382326423)
XLA Ops:
  0.0 56.8 %regrid.1 = (f32[40,2,7,16,256]{4,3,2,1,0:T(8,128)S(1)}, f32[8,14,16,256]{3,2,1,0:T(8,128)}, s32[1]{0:T(128)}) custom-call(s32[1,256]{1,0:T(1,128)} %bitcast.29, s32[256]{0:T(256)} %owner_hbm.1, f32[14]{0:T(128)} %scale_hbm.1, f32[8,14,16,256]{3,2,1,0:T(8,128)} %bitcast.26, f32[8,16,256]{2,1,0:T(8,128)} %bitcast.28, f32[8,3,16,256]{3,2,1,0:T(8,128)} %bitcast.27), custom_call_target="tpu_custom_call" | custom-call | tf_op jit(solution)/shard_map/regrid/pallas_call | solution.py:457
  56.8 0.0 copy-start
  56.8 3.6 %placed.1 = f32[40,2,7,16,256]{4,3,2,1,0:T(8,128)} custom-call(f32[40,2,7,16,256]{4,3,2,1,0:T(8,128)S(1)} %get-tuple-element.36.held), custom_call_target="tpu_custom_call" | custom-call | tf_op jit(solution)/shard_map/placed/pallas_call | solution.py:516
  60.4 0.0 copy-done
  60.4 0.6 while.10
Async XLA Ops:
  56.8 3.6 %copy-start = (s32[256]{0:T(256)S(1)}, s32[256]{0:T(256)}, u32[]{:S(2)}) copy-start(s32[256]{0:T(256)} %owner_hbm.1) | copy-start | bytes 3076

commit v7 on v6

--- a/solution.py
+++ b/solution.py
@@ -390,8 +390,10 @@
         def store_near(h, value):
             out[boxes + h, core, t, rows] = value
 
-        pick(part, FINAL + (1 - core) * 32, homes, store_far)
-        back(fin.at[part], out.at[pl.ds(boxes, homes), core, t, rows]).start()
+        some = homes // 2
+        for lead in (0, some):
+            pick(part, FINAL + (1 - core) * 32 + lead, some, lambda h, value, lead=lead: store_far(lead + h, value))
+            back(fin.at[part, pl.ds(lead, some)], out.at[pl.ds(boxes + lead, some), core, t, rows]).start()
         pick(part, FINAL + core * 32, homes, store_near)
 
     steps = (first, middle(1), middle(2), middle(3), last)

time: 61.2 us -> 61.1 us (level)
  no operation moved by 1% of the time
where the time goes in v7:
time: 61.1 us; the launch traced here: 61 us
  Pallas kernels  60.4 us (99%)
    pallas_call x1, Pallas kernels, regrid(): pl.pallas_call(functools.partial(regrid_kernel, fields, boxes, homes), ou...  56.7 us
    pallas_call x1, Pallas kernels, placed(): pl.pallas_call(place_kernel, out_shape=pltpu.HBM(held.shape, held.dtype),...  3.62 us

profile of v7, /device:TPU:1, one launch (start us, length us, event | category | flops | bytes accessed | tf_op | source)
XLA Modules:
  0.0 61.0 jit_solution(4038693201779301337)
XLA Ops:
  0.0 56.7 %regrid.1 = (f32[40,2,7,16,256]{4,3,2,1,0:T(8,128)S(1)}, f32[8,14,16,256]{3,2,1,0:T(8,128)}, s32[1]{0:T(128)}) custom-call(s32[1,256]{1,0:T(1,128)} %bitcast.29, s32[256]{0:T(256)} %owner_hbm.1, f32[14]{0:T(128)} %scale_hbm.1, f32[8,14,16,256]{3,2,1,0:T(8,128)} %bitcast.26, f32[8,16,256]{2,1,0:T(8,128)} %bitcast.28, f32[8,3,16,256]{3,2,1,0:T(8,128)} %bitcast.27), custom_call_target="tpu_custom_call" | custom-call | tf_op jit(solution)/shard_map/regrid/pallas_call | solution.py:459
  56.8 0.0 copy-start
  56.8 3.6 %placed.1 = f32[40,2,7,16,256]{4,3,2,1,0:T(8,128)} custom-call(f32[40,2,7,16,256]{4,3,2,1,0:T(8,128)S(1)} %get-tuple-element.36.held), custom_call_target="tpu_custom_call" | custom-call | tf_op jit(solution)/shard_map/placed/pallas_call | solution.py:518
  60.4 0.0 copy-done
  60.4 0.6 while.10
Async XLA Ops:
  56.8 3.6 %copy-start = (s32[256]{0:T(256)S(1)}, s32[256]{0:T(256)}, u32[]{:S(2)}) copy-start(s32[256]{0:T(256)} %owner_hbm.1) | copy-start | bytes 3076
